TPU v7x, 512 devices: a whole 4x8x8 slice. The times are simulated.
512 devices in a mesh: group: 32 (over x, z), shard: 16 (over y, core).
Axes of the slice: x: 4, y: 8, z: 8, core: 2. Of those that a mesh axis runs over, the one named last changes fastest.
Arguments:
- tokens: bfloat16 [1024, 1024], P(('group', 'shard')), may hold values from -6 to 6
- norm_gain: float32 [1024], replicated, may hold values from 0.5 to 1.5
- qkv_weight: bfloat16 [1024, 3072], P(None, 'shard'), may hold values from -0.1875 to 0.1875
- conv_weight: float32 [4, 3072], P(None, 'shard'), may hold values from -3 to 3
- conv_state: bfloat16 [1024, 3, 3072], P('group', None, 'shard'), may hold values from -6 to 6
- mesa_gates: bfloat16 [1024, 16], replicated, may hold values from -0.1875 to 0.1875
- mesa_bias: float32 [16], replicated, may hold values from -3 to 3
- ridge_term: float32 [8], replicated, may hold values from 0.5 to 2
- key_cache: bfloat16 [2048, 128, 1024], P(('group', 'shard')), may hold values from -1.25 to 1.25
- value_cache: bfloat16 [2048, 128, 1024], P(('group', 'shard')), may hold values from -6 to 6
- log_weight: bfloat16 [2048, 8, 128], P(('group', 'shard'))
- page_owner: int32 [2048], P(('group', 'shard')), may hold values from 0 to 63, as said below
- page_fill: int32 [2048], P(('group', 'shard')), may hold values from 1 to 128, as said below
- out_weight: bfloat16 [1024, 1024], P('shard'), may hold values from -0.1875 to 0.1875
- mlp_gain: float32 [1024], replicated, may hold values from 0.5 to 1.5
- gate_weight: bfloat16 [1024, 2816], P(None, 'shard'), may hold values from -0.1875 to 0.1875
- up_weight: bfloat16 [1024, 2816], P(None, 'shard'), may hold values from -0.1875 to 0.1875
- down_weight: bfloat16 [2816, 1024], P('shard'), may hold values from -0.109375 to 0.109375
Outputs:
- retrieved: bfloat16 [1024, 1024], P(('group', 'shard'))
- layer_out: bfloat16 [1024, 1024], P(('group', 'shard'))
Inputs may be any that keep to these rules, and one draw needn't show every extreme that they name: `page_owner`: slots of a pair of groups (groups 2p and 2p + 1) belong to that pair's requests: 0 to 31 are group 2p's requests in row order, 32 to 63 group 2p + 1's. Every slot is owned, every request owns one or more slots, and a request's slots may lie on any device of either group of its pair. `page_fill`: tokens stored from the start of the slot; only a request's last page may be partly filled.
All inputs are finite; a program needn't handle non-finite values.
Results may differ from a plain program's by a relative error of at most 0.0085.
Values may be sent and summed in bfloat16 or wider, within the bound.
A program may use at most 64 MiB of HBM per device.

v0:
```python
import jax
import jax.numpy as jnp
from jax import lax
from jax.sharding import PartitionSpec as P

ITERS = 4


precise = lax.Precision.HIGHEST


def partner(value, axis, apart):
    mask = 2**apart
    pairs = [(source, source ^ mask) for source in range(lax.axis_size(axis))]
    return lax.ppermute(value, axis, pairs)


def scaled_norm(row_vals, gain_vec):
    wide_rows = row_vals.astype(jnp.float32)
    factor = lax.rsqrt(jnp.mean(wide_rows * wide_rows, axis=-1, keepdims=True) + 1e-05)
    return (wide_rows * factor * gain_vec).astype(jnp.bfloat16)


def unit_rows(vectors):
    return vectors * lax.rsqrt(jnp.sum(vectors * vectors, axis=-1, keepdims=True) + 1e-06)


def slot_weights(owner_hot, decay_rows, log_weight, page_fill):
    page_len = log_weight.shape[2]
    slot_decay = jnp.dot(owner_hot, decay_rows, precision=precise)
    live_mask = (jnp.arange(page_len)[None, :] < page_fill[:, None]).astype(jnp.float32)
    return slot_decay[:, :, None] * jnp.exp(log_weight.astype(jnp.float32)) * live_mask[:, None, :]


def slot_terms(key_rows, source_rows, owner_hot, slot_weight, directions):
    slot_count, page_len, width_all = key_rows.shape
    head_count = slot_weight.shape[1]
    head_size = width_all // head_count
    member_count = owner_hot.shape[1]
    slot_dir = jnp.dot(owner_hot, directions.reshape(member_count, width_all), precision=precise)
    slot_dir = slot_dir.reshape(slot_count, head_count, head_size)
    key_wide = key_rows.astype(jnp.float32).reshape(slot_count, page_len, head_count, head_size)
    scores = jnp.einsum("sthd,shd->sht", key_wide, slot_dir, precision=precise)
    source_wide = source_rows.astype(jnp.float32).reshape(
        slot_count, page_len, head_count, head_size
    )
    contribution = jnp.einsum("sht,sthd->shd", slot_weight * scores, source_wide, precision=precise)
    summed = jnp.dot(owner_hot.T, contribution.reshape(slot_count, width_all), precision=precise)
    return summed.reshape(member_count, head_count, head_size)


def new_term(vectors, source_rows, strength_rows, key_new):
    return (
        strength_rows[:, :, None] * source_rows * jnp.sum(key_new * vectors, axis=-1, keepdims=True)
    )


def conjugate(query_rows, key_new, value_new, strength_rows, ridge_term, reduce_fn):
    solution = jnp.zeros_like(query_rows)
    residual = query_rows
    direction = query_rows
    res_norm = jnp.sum(residual * residual, axis=-1)
    for iteration in range(ITERS):
        image_vec = (
            reduce_fn(direction, False)
            + new_term(direction, key_new, strength_rows, key_new)
            + ridge_term[None, :, None] * direction
        )
        step_size = res_norm / jnp.sum(direction * image_vec, axis=-1)
        solution = solution + step_size[:, :, None] * direction
        residual = residual - step_size[:, :, None] * image_vec
        next_norm = jnp.sum(residual * residual, axis=-1)
        direction = residual + (next_norm / res_norm)[:, :, None] * direction
        res_norm = next_norm
    return reduce_fn(solution, True) + new_term(solution, value_new, strength_rows, key_new)


def pair_order(mine, theirs, parity):
    first = jnp.where(parity == 0, mine, theirs)
    second = jnp.where(parity == 0, theirs, mine)
    return jnp.concatenate([first, second], axis=0)


def body(
    tokens,
    norm_gain,
    qkv_weight,
    conv_weight,
    conv_state,
    mesa_gates,
    mesa_bias,
    ridge_term,
    key_cache,
    value_cache,
    log_weight,
    page_owner,
    page_fill,
    out_weight,
    mlp_gain,
    gate_weight,
    up_weight,
    down_weight,
):
    req_rows = tokens.shape[0]
    group_rows = req_rows * lax.axis_size("shard")
    head_count = ridge_term.shape[0]
    width_all = key_cache.shape[2]
    head_size = width_all // head_count
    parity = lax.axis_index("group") % 2
    normed = scaled_norm(tokens, norm_gain)
    fresh_proj = jnp.dot(
        lax.all_gather(normed, "shard", axis=0, tiled=True),
        qkv_weight,
        preferred_element_type=jnp.float32,
    )
    past_rows = conv_state.astype(jnp.float32)
    pre_conv = (
        conv_weight[3] * fresh_proj
        + conv_weight[0] * past_rows[:, 0]
        + conv_weight[1] * past_rows[:, 1]
        + conv_weight[2] * past_rows[:, 2]
    )
    mixed_cols = jax.nn.silu(pre_conv).astype(jnp.bfloat16)
    home_rows = lax.all_to_all(mixed_cols, "shard", split_axis=0, concat_axis=1, tiled=True)
    split_rows = home_rows.astype(jnp.float32).reshape(req_rows, 3, head_count, head_size)
    query_home = unit_rows(split_rows[:, 0])
    key_home = unit_rows(split_rows[:, 1])
    value_home = split_rows[:, 2]
    gate_vals = jax.nn.sigmoid(
        jnp.dot(normed, mesa_gates, preferred_element_type=jnp.float32) + mesa_bias
    )
    decay_home = gate_vals[:, :head_count]
    strength_home = gate_vals[:, head_count:]
    owner_hot = (page_owner[:, None] == jnp.arange(2 * group_rows)[None, :]).astype(jnp.float32)
    stored = {}

    def cache_pass(directions, decay_grp, with_values):
        far_dirs, far_decay = partner((directions, decay_grp), "group", 0)
        pair_dirs = pair_order(directions, far_dirs, parity)
        pair_decay = pair_order(decay_grp, far_decay, parity)
        if "weight" not in stored:
            stored["weight"] = slot_weights(owner_hot, pair_decay, log_weight, page_fill)
        source_rows = value_cache if with_values else key_cache
        summed = slot_terms(key_cache, source_rows, owner_hot, stored["weight"], pair_dirs)
        mine = jnp.where(parity == 0, summed[:group_rows], summed[group_rows:])
        theirs = jnp.where(parity == 0, summed[group_rows:], summed[:group_rows])
        returned = partner(theirs, "group", 0)
        return mine + returned

    def reduce_home(vectors, with_values):
        directions, decay_grp = (
            lax.all_gather(vectors, "shard", axis=0, tiled=True),
            lax.all_gather(decay_home, "shard", axis=0, tiled=True),
        )
        return lax.psum_scatter(
            cache_pass(directions, decay_grp, with_values), "shard", scatter_dimension=0, tiled=True
        )

    found = conjugate(query_home, key_home, value_home, strength_home, ridge_term, reduce_home)
    retrieved = found.reshape(req_rows, width_all).astype(jnp.bfloat16)
    columns = lax.all_to_all(retrieved, "shard", split_axis=1, concat_axis=0, tiled=True)
    attended = lax.psum_scatter(
        jnp.dot(columns, out_weight, preferred_element_type=jnp.float32),
        "shard",
        scatter_dimension=0,
        tiled=True,
    )
    mid_rows = (tokens.astype(jnp.float32) + attended).astype(jnp.bfloat16)
    mlp_in = scaled_norm(mid_rows, mlp_gain)
    piece_rows = lax.all_gather(mlp_in, "shard", axis=0, tiled=True)
    gate_part = jnp.dot(piece_rows, gate_weight, preferred_element_type=jnp.float32)
    up_part = jnp.dot(piece_rows, up_weight, preferred_element_type=jnp.float32)
    hidden_rows = (jax.nn.silu(gate_part) * up_part).astype(jnp.bfloat16)
    down_part = lax.psum_scatter(
        jnp.dot(hidden_rows, down_weight, preferred_element_type=jnp.float32),
        "shard",
        scatter_dimension=0,
        tiled=True,
    )
    layer_out = (mid_rows.astype(jnp.float32) + down_part).astype(jnp.bfloat16)
    return (retrieved, layer_out)


def solution(mesh):
    return jax.shard_map(
        body,
        mesh=mesh,
        in_specs=(
            P(("group", "shard"), None),
            P(),
            P(None, "shard"),
            P(None, "shard"),
            P("group", None, "shard"),
            P(),
            P(),
            P(),
            P(("group", "shard"), None, None),
            P(("group", "shard"), None, None),
            P(("group", "shard"), None, None),
            P(("group", "shard")),
            P(("group", "shard")),
            P("shard", None),
            P(),
            P(None, "shard"),
            P(None, "shard"),
            P("shard", None),
        ),
        out_specs=(P(("group", "shard"), None), P(("group", "shard"), None)),
        check_vma=False,
    )
```

profile of v0, /device:TPU:1, one launch (start us, length us, event | category | flops | bytes accessed | tf_op | source)
XLA Modules:
  0.0 783.0 jit_solution(7764373445284142438)
XLA Ops:
  7.2 1.0 convert_element_type.74
  8.3 0.8 fusion.150
  9.1 21.0 %all-gather.1 = bf16[16,2,1024]{2,1,0:T(2,128)(2,1)S(1)} all-gather(bf16[1,2,1024]{2,1,0:T(2,128)(2,1)S(1)} %fusion.150), channel_id=1, replica_groups=mesh['group'=32,'shard'=16] {'shard'}, dimensions={0}, use_global_device_ids=true | all-gather | bytes 69632 | tf_op jit(solution)/shard_map/all_gather | solution.py:112
  30.1 0.8 fusion.125
  30.9 1.2 multiply_convert_fusion
  32.8 3.4 all-to-all-start
  36.3 1.0 fusion.18
  37.3 17.3 %all-gather = f32[16,2,8]{2,1,0:T(2,128)S(1)} all-gather(f32[1,2,8]{2,1,0:T(2,128)S(1)} %get-tuple-element.41), channel_id=1, replica_groups=mesh['group'=32,'shard'=16] {'shard'}, dimensions={0}, use_global_device_ids=true | all-gather | bytes 1088 | tf_op jit(solution)/shard_map/all_gather | solution.py:153
  54.7 3.0 collective-permute-start
  58.4 1.3 copy.76
  59.7 1.8 copy.44
  61.8 15.9 %all_gather.26 = f32[32,8,128]{2,1,0:T(8,128)S(1)} all-gather(f32[2,8,128]{2,1,0:T(8,128)S(1)} %fusion.92), channel_id=1, replica_groups=mesh['group'=32,'shard'=16] {'shard'}, dimensions={0}, use_global_device_ids=true | all-gather | bytes 139264 | tf_op jit(solution)/shard_map/all_gather | solution.py:152
  77.7 2.2 collective-permute-start.1
  80.8 3.8 collective-permute-done.1
  84.8 0.9 fusion.75
  85.8 0.9 fusion.26
  87.2 2.2 collective-permute-start.2
  89.4 3.4 collective-permute-done.2
  93.6 59.5 %reduce-scatter.6.cloned.1.call-done = f32[2,8,128]{2,1,0:T(8,128)} async-done(((f32[32,8,128]{2,1,0:T(8,128)}), f32[2,8,128]{2,1,0:T(8,128)}) %reduce-scatter.6.cloned.1.call-update) | async-done | bytes 8208 | tf_op jit(solution)/shard_map/reduce_scatter | solution.py:155
  153.2 0.9 multiply_reduce_fusion.6
  155.1 16.7 %all_gather.27 = f32[32,8,128]{2,1,0:T(8,128)S(1)} all-gather(f32[2,8,128]{2,1,0:T(8,128)S(1)} %multiply_add_fusion.5), channel_id=1, replica_groups=mesh['group'=32,'shard'=16] {'shard'}, dimensions={0}, use_global_device_ids=true | all-gather | bytes 139264 | tf_op jit(solution)/shard_map/all_gather | solution.py:152
  171.7 3.3 collective-permute-start.3
  175.0 3.6 collective-permute-done.3
  178.8 0.9 fusion.73
  179.8 0.9 fusion.24
  181.2 3.3 collective-permute-start.4
  184.5 2.4 collective-permute-done.4
  187.7 57.6 %reduce-scatter.8.cloned.1.call-done = f32[2,8,128]{2,1,0:T(8,128)} async-done(((f32[32,8,128]{2,1,0:T(8,128)}), f32[2,8,128]{2,1,0:T(8,128)}) %reduce-scatter.8.cloned.1.call-update) | async-done | bytes 8208 | tf_op jit(solution)/shard_map/reduce_scatter | solution.py:155
  245.2 1.0 multiply_reduce_fusion.4
  246.5 16.7 %all_gather.28 = f32[32,8,128]{2,1,0:T(8,128)S(1)} all-gather(f32[2,8,128]{2,1,0:T(8,128)S(1)} %multiply_add_fusion.3), channel_id=1, replica_groups=mesh['group'=32,'shard'=16] {'shard'}, dimensions={0}, use_global_device_ids=true | all-gather | bytes 139264 | tf_op jit(solution)/shard_map/all_gather | solution.py:152
  263.2 3.3 collective-permute-start.5
  266.5 3.5 collective-permute-done.5
  270.3 0.9 fusion.71
  271.3 0.9 fusion.22
  272.7 3.3 collective-permute-start.6
  276.0 2.4 collective-permute-done.6
  279.4 57.3 %reduce-scatter.10.cloned.1.call-done = f32[2,8,128]{2,1,0:T(8,128)} async-done(((f32[32,8,128]{2,1,0:T(8,128)}), f32[2,8,128]{2,1,0:T(8,128)}) %reduce-scatter.10.cloned.1.call-update) | async-done | bytes 8208 | tf_op jit(solution)/shard_map/reduce_scatter | solution.py:155
  336.7 0.8 multiply_reduce_fusion.2
  337.8 16.7 %all_gather.29 = f32[32,8,128]{2,1,0:T(8,128)S(1)} all-gather(f32[2,8,128]{2,1,0:T(8,128)S(1)} %multiply_add_fusion.1), channel_id=1, replica_groups=mesh['group'=32,'shard'=16] {'shard'}, dimensions={0}, use_global_device_ids=true | all-gather | bytes 139264 | tf_op jit(solution)/shard_map/all_gather | solution.py:152
  354.5 3.4 collective-permute-start.7
  358.0 3.5 collective-permute-done.7
  361.8 0.9 fusion.69
  362.8 0.9 fusion.28
  364.2 3.3 collective-permute-start.8
  367.5 2.7 collective-permute-done.8
  371.2 56.8 %reduce-scatter.12.cloned.1.call-done = f32[2,8,128]{2,1,0:T(8,128)} async-done(((f32[32,8,128]{2,1,0:T(8,128)}), f32[2,8,128]{2,1,0:T(8,128)}) %reduce-scatter.12.cloned.1.call-update) | async-done | bytes 8208 | tf_op jit(solution)/shard_map/reduce_scatter | solution.py:155
  428.0 0.8 multiply_reduce_fusion
  429.0 16.7 %all_gather.30 = f32[32,8,128]{2,1,0:T(8,128)S(1)} all-gather(f32[2,8,128]{2,1,0:T(8,128)S(1)} %multiply_add_fusion), channel_id=1, replica_groups=mesh['group'=32,'shard'=16] {'shard'}, dimensions={0}, use_global_device_ids=true | all-gather | bytes 139264 | tf_op jit(solution)/shard_map/all_gather | solution.py:152
  445.7 3.4 collective-permute-start.9
  449.1 3.4 collective-permute-done.9
  452.8 0.9 fusion.67
  453.8 0.9 fusion.19
  455.2 3.3 collective-permute-start.10
  458.5 2.4 collective-permute-done.10
  461.9 57.5 %reduce-scatter.14.cloned.1.call-done = f32[2,8,128]{2,1,0:T(8,128)} async-done(((f32[32,8,128]{2,1,0:T(8,128)}), f32[2,8,128]{2,1,0:T(8,128)}) %reduce-scatter.14.cloned.1.call-update) | async-done | bytes 8208 | tf_op jit(solution)/shard_map/reduce_scatter | solution.py:155
  520.2 13.7 %all_to_all.29 = bf16[2,16,64]{2,0,1:T(2,128)(2,1)S(1)} all-to-all(bf16[2,16,64]{2,0,1:T(2,128)(2,1)S(1)} %copy.42), channel_id=1, replica_groups=mesh['group'=32,'shard'=16] {'shard'}, dimensions={1} | all-to-all | bytes 8192 | tf_op jit(solution)/shard_map/all_to_all | solution.py:161
  533.9 0.8 fusion.127
  534.8 1.3 dynamic-slice
  536.8 107.0 %all-reduce.5.cloned.1.call-done = f32[32,1024]{1,0:T(8,128)} async-done(((f32[32,1024]{1,0:T(8,128)}), f32[32,1024]{1,0:T(8,128)}) %all-reduce.5.cloned.1.call-update) | async-done | bytes 131088
  643.9 0.9 fusion.87
  644.8 15.8 %all-gather.2 = bf16[16,2,1024]{2,1,0:T(2,128)(2,1)S(1)} all-gather(bf16[1,2,1024]{2,1,0:T(2,128)(2,1)S(1)} %fusion.98), channel_id=1, replica_groups=mesh['group'=32,'shard'=16] {'shard'}, dimensions={0}, use_global_device_ids=true | all-gather | bytes 69632 | tf_op jit(solution)/shard_map/all_gather | solution.py:170
  660.9 1.1 fusion.9
  662.7 112.1 %all-reduce.7.cloned.1.call-done = f32[32,1024]{1,0:T(8,128)} async-done(((f32[32,1024]{1,0:T(8,128)}), f32[32,1024]{1,0:T(8,128)}) %all-reduce.7.cloned.1.call-update) | async-done | bytes 131088
  774.8 1.4 fusion.90
  (130 shorter events, 14.7 us)
Async XLA Ops:
  7.2 446.6 %copy-start = (bf16[4,128,1024]{2,1,0:T(8,128)(2,1)S(1)}, bf16[4,128,1024]{2,1,0:T(8,128)(2,1)}, u32[]{:S(2)}) copy-start(bf16[4,128,1024]{2,1,0:T(8,128)(2,1)} %param.27) | copy-start | bytes 3145732
  7.2 1.0 copy-start.8
  7.2 51.2 %copy-start.1 = (bf16[4,128,1024]{2,1,0:T(8,128)(2,1)S(1)}, bf16[4,128,1024]{2,1,0:T(8,128)(2,1)}, u32[]{:S(2)}) copy-start(bf16[4,128,1024]{2,1,0:T(8,128)(2,1)} %param.26) | copy-start | bytes 3145732
  32.8 28.7 %all-to-all-start = ((bf16[16,2,192]{2,1,0:T(2,128)(2,1)}), bf16[16,2,192]{2,1,0:T(2,128)(2,1)S(1)}, u32[]{:S(2)}, u32[]{:S(2)}) async-start(bf16[16,2,192]{2,1,0:T(2,128)(2,1)} %all_to_all.22), calls=%async_computation | async-start | bytes 32768 | tf_op jit(solution)/shard_map/all_to_all | solution.py:124
  36.3 116.9 %reduce-scatter.6.cloned.1.call-start = ((), (), s32[]{:S(2)}) async-start(), calls=%async_computation.7 | async-start | bytes 139264 | tf_op jit(solution)/shard_map/reduce_scatter | solution.py:155
  54.7 6.8 collective-permute-start
  57.7 0.7 copy-start.13
  77.7 6.8 collective-permute-start.1
  79.9 0.7 copy-start.7
  84.8 0.9 copy-start.5
  87.2 5.7 collective-permute-start.2
  93.6 151.7 %reduce-scatter.8.cloned.1.call-start = ((), (), s32[]{:S(2)}) async-start(), calls=%async_computation.8 | async-start | bytes 139264 | tf_op jit(solution)/shard_map/reduce_scatter | solution.py:155
  93.6 59.5 %copy-start.9 = (f32[8]{0:T(128)S(1)}, f32[8]{0:T(128)}, u32[]{:S(2)}) copy-start(f32[8]{0:T(128)} %param.25) | copy-start | bytes 100
  154.1 0.7 copy-start.10
  171.7 6.8 collective-permute-start.3
  181.2 5.7 collective-permute-start.4
  187.6 149.1 %reduce-scatter.10.cloned.1.call-start = ((), (), s32[]{:S(2)}) async-start(), calls=%async_computation.9 | async-start | bytes 139264 | tf_op jit(solution)/shard_map/reduce_scatter | solution.py:155
  245.2 1.0 copy-start.11
  263.2 6.8 collective-permute-start.5
  272.7 5.7 collective-permute-start.6
  279.1 148.9 %reduce-scatter.12.cloned.1.call-start = ((), (), s32[]{:S(2)}) async-start(), calls=%async_computation.10 | async-start | bytes 139264 | tf_op jit(solution)/shard_map/reduce_scatter | solution.py:155
  354.5 7.0 collective-permute-start.7
  364.2 6.0 collective-permute-start.8
  370.9 148.5 %reduce-scatter.14.cloned.1.call-start = ((), (), s32[]{:S(2)}) async-start(), calls=%async_computation.11 | async-start | bytes 139264 | tf_op jit(solution)/shard_map/reduce_scatter | solution.py:155
  445.7 6.8 collective-permute-start.9
  455.2 5.7 collective-permute-start.10
  461.5 72.4 %copy-start.6 = (bf16[64,1024]{1,0:T(8,128)(2,1)S(1)}, bf16[64,1024]{1,0:T(8,128)(2,1)}, u32[]{:S(2)}) copy-start(bf16[64,1024]{1,0:T(8,128)(2,1)} %param.31) | copy-start | bytes 393220
  461.6 182.3 %all-reduce.5.cloned.1.call-start = ((), (), s32[]{:S(2)}) async-start(), calls=%async_computation.12 | async-start | bytes 262144
  520.1 140.6 %copy-start.2 = (bf16[1024,176]{0,1:T(8,128)(2,1)S(1)}, bf16[1024,176]{0,1:T(8,128)(2,1)}, u32[]{:S(2)}) copy-start(bf16[1024,176]{0,1:T(8,128)(2,1)} %param.33) | copy-start | bytes 1081348
  533.9 110.8 %copy-start.12 = (f32[1024]{0:T(1024)S(1)}, f32[1024]{0:T(1024)}, u32[]{:S(2)}) copy-start(f32[1024]{0:T(1024)} %param.32) | copy-start | bytes 12292
  534.8 240.0 %all-reduce.7.cloned.1.call-start = ((), (), s32[]{:S(2)}) async-start(), calls=%async_computation.13 | async-start | bytes 262144
  534.8 126.1 %copy-start.3 = (bf16[176,1024]{1,0:T(8,128)(2,1)S(1)}, bf16[176,1024]{1,0:T(8,128)(2,1)}, u32[]{:S(2)}) copy-start(bf16[176,1024]{1,0:T(8,128)(2,1)} %param.35) | copy-start | bytes 1081348
  534.8 126.1 %copy-start.4 = (bf16[1024,176]{0,1:T(8,128)(2,1)S(1)}, bf16[1024,176]{0,1:T(8,128)(2,1)}, u32[]{:S(2)}) copy-start(bf16[1024,176]{0,1:T(8,128)(2,1)} %param.34) | copy-start | bytes 1081348
Sparse Core Ops, SparseCore 0:
  93.7 59.4 reduce-scatter.5
  187.7 57.4 reduce-scatter.7
  279.2 57.4 reduce-scatter.9
  371.0 56.9 reduce-scatter.11
  461.7 57.6 reduce-scatter.13
  534.9 108.9 all-reduce.4
  662.2 112.5 all-reduce.6
where the time goes:
time: 784 us; the launch traced here: 783 us
  waiting for transfers between devices  539 us (69%)
  blocking collectives  151 us (19%)
  starting transfers between devices  37.7 us (5%)
  matrix products  16.8 us (2%)
  between operations  15.3 us (2%)
  other arithmetic  14.5 us (2%)
  local copies, waits for them, and re-layouts  9.11 us (1%)
    reduce_scatter x5, waiting for transfers between devices, reduce_home(): lax.psum_scatter(cache_pass(directions, decay_grp, with_values), 'shard',...  289 us
    unnamed x9, waiting for transfers between devices  219 us
    all_gather x5, blocking collectives, reduce_home(): lax.all_gather(vectors, 'shard', axis=0, tiled=True)  82.7 us
    ppermute x11, starting transfers between devices, partner(): return lax.ppermute(value, axis, pairs)  34 us
    ppermute x11, waiting for transfers between devices, partner(): return lax.ppermute(value, axis, pairs)  31.1 us
    all_gather x1, blocking collectives, body(): lax.all_gather(normed, 'shard', axis=0, tiled=True)  21 us
    all_gather x1, blocking collectives, reduce_home(): lax.all_gather(decay_home, 'shard', axis=0, tiled=True)  17.3 us
    all_gather x1, blocking collectives, body(): piece_rows = lax.all_gather(mlp_in, 'shard', axis=0, tiled=True)  15.8 us
  transfers between devices with their start and end apart: 19, of which 17 were waited for; matrix products, arithmetic and copies ran while one was open for 1% of the time, Pallas kernels for 0%

commit v1 on v0

v1 whole, which is shorter than its diff:
```python
import functools

import jax
import jax.numpy as jnp
from jax import lax
from jax.experimental import pallas as pl
from jax.experimental.pallas import tpu as pltpu
from jax.sharding import PartitionSpec as P

MESH = pl.DeviceIdType.MESH
F32 = jnp.float32
BF16 = jnp.bfloat16
ITERS = 4


def iota(shape, dim):
    return lax.broadcasted_iota(jnp.int32, shape, dim)


def mm(a, b):
    return jnp.dot(a, b, preferred_element_type=F32)


def mm_nt(a, b):
    return lax.dot_general(a, b, (((1,), (1,)), ((), ())), preferred_element_type=F32)


def split(v):
    hi = v.astype(BF16)
    lo = (v - hi.astype(F32)).astype(BF16)
    return hi, lo


def silu(v):
    return v / (1.0 + jnp.exp(-v))


def row_norm(wide, gain):
    factor = lax.rsqrt(jnp.mean(wide * wide, axis=-1, keepdims=True) + 1e-05)
    return (wide * factor * gain).astype(BF16)


def unit_rows(v):
    return v * lax.rsqrt(jnp.sum(v * v, axis=-1, keepdims=True) + 1e-06)


def rowsum(v):
    return jnp.sum(v, axis=-1, keepdims=True)


def kernel(
    tok_ref, ngain_ref, qkvw_hbm, convw_ref, convs_hbm, mgate_ref, mbias_ref, ridge_ref,
    key_hbm, val_hbm, logw_ref, owner_ref, fill_ref, outw_hbm, mgain_ref, gatew_hbm, upw_hbm, downw_hbm,
    ret_ref, lay_ref,
    qkvw, convs, outw, gatew, upw, downw,
    kall, vall, tokall, xrows, wo_src, wo_all, wmask,
    usrc, uall, gall, ohd, ohall, ohs,
    csrc, call, fsrc, fall, psrc, hall, msrc, mall, nsrc, nall,
    lsem, osem, ssem, rsem,
):
    g = lax.axis_index("group")
    s = lax.axis_index("shard")
    par = g % 2
    base = g - par
    y = s // 2
    c = s % 2
    q = par * 2 + c

    def local(src, dst, sem):
        cp = pltpu.make_async_copy(src, dst, sem)
        cp.start()
        return cp

    def remote(src, dst, send, recv, dev):
        pltpu.make_async_remote_copy(
            src_ref=src, dst_ref=dst, send_sem=send, recv_sem=recv,
            device_id=dev, device_id_type=MESH,
        ).start()

    def done(ref, sem):
        pltpu.make_async_copy(ref, ref, sem).wait()

    def each(n, fn):
        def step(k, carry):
            fn(k)
            return carry
        lax.fori_loop(0, n, step, 0)

    def team(t):
        return base + t // 2, 2 * y + t % 2

    def line(k):
        return g, 2 * ((y + k) % 8) + c

    bar = pltpu.get_barrier_semaphore()
    rank = par * 16 + s

    def greet(k):
        to = (rank + k + 1) % 32
        pl.semaphore_signal(bar, inc=1, device_id=(base + to // 16, to % 16), device_id_type=MESH)

    each(31, greet)

    c_conv = local(convs_hbm, convs, lsem.at[0])
    c_qkv = local(qkvw_hbm, qkvw, lsem.at[1])
    mine = pl.ds(pl.multiple_of(q * 256, 256), 256)
    local(key_hbm.at[:, :, mine], kall.at[pl.ds(q * 4, 4)], rsem.at[0])
    c_gate = local(gatew_hbm, gatew, lsem.at[2])
    c_up = local(upw_hbm, upw, lsem.at[3])
    c_down = local(downw_hbm, downw, lsem.at[4])
    local(outw_hbm, outw.at[c], rsem.at[1])
    local(val_hbm.at[:, :, mine], vall.at[pl.ds(q * 4, 4)], rsem.at[2])
    local(tok_ref, tokall.at[s], rsem.at[3])

    row8 = iota((8, 128), 0)
    lane8 = iota((8, 128), 1)
    slot8 = row8 % 4

    def pick(ref):
        return jnp.where(
            slot8 == 0, ref[0], jnp.where(slot8 == 1, ref[1], jnp.where(slot8 == 2, ref[2], ref[3]))
        )

    live = lane8 < pick(fill_ref)
    own8 = pick(owner_ref).astype(F32)
    logw = logw_ref[...].astype(F32)
    for t in range(4):
        rows = [logw[j, 2 * t + h : 2 * t + h + 1, :] for h in range(2) for j in range(4)]
        wo_src[t, 0:8, :] = jnp.where(live, jnp.exp(jnp.concatenate(rows, axis=0)), 0.0)
        wo_src[t, 8:16, :] = own8
    c_conv.wait()
    past = jnp.zeros((32, 192), F32)
    for k in range(3):
        past = past + convw_ref[k : k + 1, :] * convs[k].astype(F32)

    pl.semaphore_wait(bar, 31)

    def send_tok(k):
        to = (s + k + 1) % 16
        remote(tok_ref, tokall.at[s], ssem.at[0], rsem.at[3], (g, to))

    each(15, send_tok)
    local(wo_src.at[q], wo_all.at[q], rsem.at[4])

    def send_wo(k):
        t = (q + k + 1) % 4
        remote(wo_src.at[t], wo_all.at[q], ssem.at[1], rsem.at[4], team(t))

    each(3, send_wo)

    def send_key(k):
        t = (q + k + 1) % 4
        cols = pl.ds(pl.multiple_of(t * 256, 256), 256)
        remote(key_hbm.at[:, :, cols], kall.at[pl.ds(q * 4, 4)], ssem.at[2], rsem.at[0], team(t))

    each(3, send_key)

    c_qkv.wait()
    done(tokall, rsem.at[3])
    for i in range(16):
        xrows[2 * i : 2 * i + 2, :] = tokall[i].astype(F32)
    normed = row_norm(xrows[...], ngain_ref[...])
    fresh = mm(normed, qkvw[...])
    pre = convw_ref[3:4, :] * fresh + past
    mixed = silu(pre).astype(BF16).astype(F32)
    lane16 = iota((16, 128), 1)
    low16 = lane16 < 64
    a = mixed[:, 0:128]
    b = mixed[:, 64:192]

    def fold(lower, upper):
        return jnp.where(low16, lower, upper).astype(BF16)

    usrc[0] = fold(a[0:16], pltpu.roll(a[16:32], 64, 1))
    usrc[1] = fold(pltpu.roll(a[0:16], 64, 1), a[16:32])
    usrc[2] = fold(pltpu.roll(b[0:16], 64, 1), b[16:32])
    for j in range(3):
        unit = 3 * s + j
        part = unit % 16
        tq = part // 4
        slot = par * 12 + (unit // 16) * 4 + part % 4
        tg = base + tq // 2

        def send_unit(k, j=j, tq=tq, slot=slot, tg=tg):
            to = 2 * ((y + k + 1) % 8) + tq % 2
            remote(usrc.at[j], uall.at[slot], ssem.at[3], rsem.at[5], (tg, to))

        each(7, send_unit)

        @pl.when(tq == q)
        def _(j=j, slot=slot):
            local(usrc.at[j], uall.at[slot], rsem.at[5])

        @pl.when(tq != q)
        def _(j=j, slot=slot, tg=tg, tq=tq):
            remote(usrc.at[j], uall.at[slot], osem.at[j], rsem.at[5], (tg, 2 * y + tq % 2))

    gates = jax.nn.sigmoid(mm(normed, mgate_ref[...]) + mbias_ref[...])
    gall[par, :, 0:16] = gates
    remote(gall.at[par], gall.at[par], ssem.at[4], rsem.at[6], (base + 1 - par, s))

    done(wo_all, rsem.at[4])
    row32 = iota((32, 128), 0)
    lane32 = iota((32, 128), 1)
    first = (row32 // 4) % 2 == 0
    own32 = wo_all[:, 8:16, :].reshape(32, 128)
    hot = (own32 == (lane32 % 64).astype(F32)) & ((row32 // 4) % 2 == lane32 // 64)
    ohd[...] = hot.astype(F32).astype(BF16)
    local(ohd, ohall.at[y], rsem.at[7])

    def send_oh(k):
        remote(ohd, ohall.at[y], ssem.at[5], rsem.at[7], line(k + 1))

    each(7, send_oh)
    w32 = wo_all[:, 0:8, :].reshape(32, 128)
    slot32 = (row32 // 8) * 4 + row32 % 4
    for p in range(16):
        wmask[:, 128 * p : 128 * p + 128] = jnp.where(slot32 == p, w32, 0.0)

    done(uall, rsem.at[5])
    done(gall.at[0], rsem.at[6])

    def send_val(k):
        t = (q + k + 1) % 4
        cols = pl.ds(pl.multiple_of(t * 256, 256), 256)
        remote(val_hbm.at[:, :, cols], vall.at[pl.ds(q * 4, 4)], ssem.at[6], rsem.at[2], team(t))

    each(3, send_val)
    remote(outw_hbm, outw.at[c], ssem.at[7], rsem.at[1], (g, 2 * y + 1 - c))

    def unfold(kind):
        blocks = []
        for h in range(2):
            for p in range(2):
                left = uall[p * 12 + kind * 4 + 2 * h].astype(F32)
                right = uall[p * 12 + kind * 4 + 2 * h + 1].astype(F32)
                blocks.append(jnp.where(low16, left, pltpu.roll(right, 64, 1)))
                blocks.append(jnp.where(low16, pltpu.roll(left, 64, 1), right))
        return jnp.concatenate(blocks, axis=0)

    query = unit_rows(unfold(0))
    knew = unit_rows(unfold(1))
    vnew = unfold(2)
    gboth = gall[...].reshape(64, 128)
    lane64 = iota((64, 128), 1)

    def column(at):
        halves = [rowsum(jnp.where(lane64 == at + h, gboth, 0.0)) for h in range(2)]
        return jnp.concatenate(halves, axis=0)

    decay = column(2 * q)
    strength = column(8 + 2 * q)
    rowc = iota((128, 1), 0)
    ridge = jnp.where(rowc < 64, ridge_ref[2 * q], ridge_ref[2 * q + 1])

    done(ohall, rsem.at[7])
    ohs[...] = ohall[...].reshape(256, 128).astype(F32).T.astype(BF16)
    done(kall, rsem.at[0])

    def spread(picked):
        return jnp.concatenate([jnp.where(first, picked, 0.0), jnp.where(first, 0.0, picked)], axis=1)

    def weigh(scores):
        hi, lo = split((scores[0:32] + scores[32:64]) * wmask[...])
        return jnp.concatenate([hi, lo], axis=0)

    def gathered(prod):
        both = prod[0:32] + prod[32:64]
        return jnp.where(first, both[:, 0:128], both[:, 128:256])

    def own_term(vec, source):
        return strength * source * rowsum(knew * vec)

    keys = kall[...].reshape(2048, 256)
    solution = jnp.zeros((128, 128), F32)
    residual = query
    direction = query
    res_norm = rowsum(residual * residual)
    for it in range(ITERS - 1):
        hi, lo = split(direction)
        sel = mm(ohd[...], jnp.concatenate([hi, lo], axis=1))
        lhs = jnp.concatenate([spread(sel[:, 0:128]), spread(sel[:, 128:256])], axis=0).astype(BF16)
        csrc[it] = gathered(mm(weigh(mm_nt(lhs, keys)), keys)).astype(BF16)
        local(csrc.at[it], call.at[it, y], rsem.at[8 + it])

        def send_c(k, it=it):
            remote(csrc.at[it], call.at[it, y], ssem.at[8 + it], rsem.at[8 + it], line(k + 1))

        each(7, send_c)
        near = own_term(direction, knew) + ridge * direction
        done(call.at[it], rsem.at[8 + it])
        image = decay * mm(ohs[...], call[it].reshape(256, 128)) + near
        step_size = res_norm / rowsum(direction * image)
        solution = solution + step_size * direction
        residual = residual - step_size * image
        next_norm = rowsum(residual * residual)
        direction = residual + (next_norm / res_norm) * direction
        res_norm = next_norm

    dhi, dlo = split(direction)
    xhi, xlo = split(solution)
    sel = mm(ohd[...], jnp.concatenate([dhi, dlo, xhi, xlo], axis=1))
    lhs = jnp.concatenate([spread(sel[:, 128 * i : 128 * i + 128]) for i in range(4)], axis=0).astype(BF16)
    scores = mm_nt(lhs, keys)
    dweigh = weigh(scores[0:64])
    xweigh = weigh(scores[64:128])
    fsrc[0:32, :] = gathered(mm(dweigh, keys)).astype(BF16)
    done(vall, rsem.at[2])
    values = vall[...].reshape(2048, 256)
    reads = mm(jnp.concatenate([dweigh, xweigh], axis=0), values)
    fsrc[32:64, :] = gathered(reads[0:64]).astype(BF16)
    fsrc[64:96, :] = gathered(reads[64:128]).astype(BF16)
    active = q == y // 2
    for h in range(2):
        ty = 2 * q + h

        @pl.when(ty == y)
        def _():
            local(fsrc, fall.at[y], rsem.at[11])

        @pl.when(ty != y)
        def _(h=h, ty=ty):
            remote(fsrc, fall.at[y], osem.at[3 + h], rsem.at[11], (g, 2 * ty + c))

    done(outw, rsem.at[1])

    @pl.when(active)
    def _():
        near = own_term(direction, knew) + ridge * direction
        near_d = own_term(direction, vnew)
        near_x = own_term(solution, vnew)
        done(fall, rsem.at[11])
        got = [mm(ohs[...], fall[:, 32 * i : 32 * i + 32, :].reshape(256, 128)) for i in range(3)]
        image = decay * got[0] + near
        step_size = res_norm / rowsum(direction * image)
        both = decay * got[2] + near_x + step_size * (decay * got[1] + near_d)
        found = jnp.where(y % 2 == 0, both[0:64], both[64:128]).astype(BF16)
        partial = mm(found, outw[...].reshape(128, 1024)).astype(BF16)
        for r in range(32):
            psrc[r, :, 0:1024] = partial[2 * r : 2 * r + 2, :]
            psrc[r, :, 1024:1152] = found[2 * r : 2 * r + 2, :]
        local(psrc.at[rank], hall.at[y], rsem.at[12])

        def send_p(k):
            to = (rank + k + 1) % 32
            remote(psrc.at[to], hall.at[y], ssem.at[11], rsem.at[12], (base + to // 16, to % 16))

        each(31, send_p)

    done(hall, rsem.at[12])
    attended = jnp.zeros((2, 1024), F32)
    for h in range(8):
        attended = attended + hall[h, :, 0:1024].astype(F32)
        ret_ref[:, 128 * h : 128 * h + 128] = hall[h, :, 1024:1152]
    mid = (tok_ref[...].astype(F32) + attended).astype(BF16).astype(F32)
    msrc[...] = row_norm(mid, mgain_ref[...])
    local(msrc, mall.at[s], rsem.at[13])

    def send_m(k):
        remote(msrc, mall.at[s], ssem.at[12], rsem.at[13], (g, (s + k + 1) % 16))

    each(15, send_m)
    c_gate.wait()
    c_up.wait()
    c_down.wait()
    done(mall, rsem.at[13])
    for i in range(16):
        xrows[2 * i : 2 * i + 2, :] = mall[i].astype(F32)
    rows = xrows[...].astype(BF16)
    hidden = (silu(mm(rows, gatew[...])) * mm(rows, upw[...])).astype(BF16)
    down = mm(hidden, downw[...]).astype(BF16)
    for r in range(16):
        nsrc[r] = down[2 * r : 2 * r + 2, :]
    local(nsrc.at[s], nall.at[s], rsem.at[14])

    def send_n(k):
        to = (s + k + 1) % 16
        remote(nsrc.at[to], nall.at[s], ssem.at[13], rsem.at[14], (g, to))

    each(15, send_n)
    done(nall, rsem.at[14])
    total = mid
    for i in range(16):
        total = total + nall[i].astype(F32)
    lay_ref[...] = total.astype(BF16)

    done(tokall.at[pl.ds(0, 15)], ssem.at[0])
    done(wo_all.at[pl.ds(0, 3)], ssem.at[1])
    done(kall.at[pl.ds(0, 12)], ssem.at[2])
    done(uall.at[pl.ds(0, 21)], ssem.at[3])
    done(gall.at[0], ssem.at[4])
    done(ohall.at[pl.ds(0, 7)], ssem.at[5])
    done(vall.at[pl.ds(0, 12)], ssem.at[6])
    done(outw.at[0], ssem.at[7])
    for it in range(ITERS - 1):
        done(call.at[it, pl.ds(0, 7)], ssem.at[8 + it])
    for j in range(3):
        @pl.when(((3 * s + j) % 16) // 4 != q)
        def _(j=j):
            done(usrc.at[j], osem.at[j])
    for h in range(2):
        @pl.when(2 * q + h != y)
        def _(h=h):
            done(fsrc, osem.at[3 + h])

    @pl.when(active)
    def _():
        done(psrc.at[pl.ds(0, 31)], ssem.at[11])

    @pl.when(jnp.logical_not(active))
    def _():
        pass

    done(mall.at[pl.ds(0, 15)], ssem.at[12])
    done(nall.at[pl.ds(0, 15)], ssem.at[13])


def body(
    tokens, norm_gain, qkv_weight, conv_weight, conv_state, mesa_gates, mesa_bias, ridge_term,
    key_cache, value_cache, log_weight, page_owner, page_fill, out_weight, mlp_gain,
    gate_weight, up_weight, down_weight,
):
    vm = pl.BlockSpec(memory_space=pltpu.VMEM)
    sm = pl.BlockSpec(memory_space=pltpu.SMEM)
    hb = pl.BlockSpec(memory_space=pltpu.HBM)
    v = pltpu.VMEM
    dma = pltpu.SemaphoreType.DMA
    return pl.pallas_call(
        kernel,
        name="layer",
        out_shape=(
            jax.ShapeDtypeStruct((2, 1024), BF16),
            jax.ShapeDtypeStruct((2, 1024), BF16),
        ),
        in_specs=[vm, vm, hb, vm, hb, vm, vm, sm, hb, hb, vm, sm, sm, hb, vm, hb, hb, hb],
        out_specs=(vm, vm),
        scratch_shapes=[
            v((1024, 192), BF16), v((3, 32, 192), BF16), v((2, 64, 1024), BF16),
            v((1024, 176), BF16), v((1024, 176), BF16), v((176, 1024), BF16),
            v((16, 128, 256), BF16), v((16, 128, 256), BF16),
            v((16, 2, 1024), BF16), v((32, 1024), F32),
            v((4, 16, 128), F32), v((4, 16, 128), F32), v((32, 2048), F32),
            v((3, 16, 128), BF16), v((24, 16, 128), BF16), v((2, 32, 128), F32),
            v((32, 128), BF16), v((8, 32, 128), BF16), v((128, 256), BF16),
            v((3, 32, 128), BF16), v((3, 8, 32, 128), BF16),
            v((96, 128), BF16), v((8, 96, 128), BF16),
            v((32, 2, 1152), BF16), v((8, 2, 1152), BF16),
            v((2, 1024), BF16), v((16, 2, 1024), BF16),
            v((16, 2, 1024), BF16), v((16, 2, 1024), BF16),
            dma((5,)), dma((5,)), dma((14,)), dma((15,)),
        ],
        compiler_params=pltpu.CompilerParams(
            collective_id=0, has_side_effects=True, vmem_limit_bytes=56 * 1024 * 1024
        ),
    )(
        tokens, norm_gain.reshape(1, -1), qkv_weight, conv_weight, conv_state.transpose(1, 0, 2),
        mesa_gates, mesa_bias.reshape(1, -1), ridge_term, key_cache, value_cache, log_weight,
        page_owner, page_fill, out_weight, mlp_gain.reshape(1, -1), gate_weight, up_weight, down_weight,
    )


def solution(mesh):
    return jax.shard_map(
        body,
        mesh=mesh,
        in_specs=(
            P(("group", "shard"), None),
            P(),
            P(None, "shard"),
            P(None, "shard"),
            P("group", None, "shard"),
            P(),
            P(),
            P(),
            P(("group", "shard"), None, None),
            P(("group", "shard"), None, None),
            P(("group", "shard"), None, None),
            P(("group", "shard")),
            P(("group", "shard")),
            P("shard", None),
            P(),
            P(None, "shard"),
            P(None, "shard"),
            P("shard", None),
        ),
        out_specs=(P(("group", "shard"), None), P(("group", "shard"), None)),
        check_vma=False,
    )
```

time: 784 us -> 78.3 us (0.10)
  waiting for transfers between devices: 539 us -> 0 us
  blocking collectives: 151 us -> 0 us
  Pallas kernels: 0 us -> 69.8 us
  starting transfers between devices: 37.7 us -> 0 us
  matrix products: 16.8 us -> 0 us
  between operations: 15.3 us -> 0.65 us
  other arithmetic: 14.5 us -> 0 us
    reduce_scatter x5 -> x0, waiting for transfers between devices: 289 us -> none  [reduce_home(): lax.psum_scatter(cache_pass(directions, decay_grp, with_values), 'shard',...]
    unnamed x9 -> x0, waiting for transfers between devices: 219 us -> none
    all_gather x8 -> x0, blocking collectives: 137 us -> none  [the longest x5 82.7 us: reduce_home(): lax.all_gather(vectors, 'shard', axis=0, tiled=True)]
    pallas_call x0 -> x1, Pallas kernels: none -> 69.8 us  [body(): pl.pallas_call(kernel, name='layer', out_shape=(jax.ShapeDtypeStruct((2,...]
    ppermute x11 -> x0, starting transfers between devices: 34 us -> none  [partner(): return lax.ppermute(value, axis, pairs)]
    ppermute x11 -> x0, waiting for transfers between devices: 31.1 us -> none  [partner(): return lax.ppermute(value, axis, pairs)]
    dot_general x26 -> x0, matrix products: 16.8 us -> none  [the longest x5 4.65 us: slot_terms(): jnp.einsum('sht,sthd->shd', slot_weight * scores, source_wide, precision=...]
    all_to_all x1 -> x0, blocking collectives: 13.7 us -> none  [body(): lax.all_to_all(retrieved, 'shard', split_axis=1, concat_axis=0, tiled=True)]
  transfers between devices with their start and end apart: 19 -> 0, of which waited for: 17 -> 0; matrix products, arithmetic and copies ran while one was open for 1% -> 0% of each run, Pallas kernels for 0% -> 0%
where the time goes in v1:
time: 78.3 us; the launch traced here: 78 us
  Pallas kernels  69.8 us (89%)
  local copies, waits for them, and re-layouts  7.53 us (10%)
    pallas_call x1, Pallas kernels, body(): pl.pallas_call(kernel, name='layer', out_shape=(jax.ShapeDtypeStruct((2,...  69.8 us
    unnamed x12, local copies, waits for them, and re-layouts  7.53 us

profile of v1, /device:TPU:1, one launch (start us, length us, event | category | flops | bytes accessed | tf_op | source)
XLA Modules:
  0.0 78.0 jit_solution(15542121704997489407)
XLA Ops:
  0.6 1.6 %copy.21.mgate_ref = bf16[1024,16]{1,0:T(8,128)(2,1)} copy(bf16[1024,16]{0,1:T(8,128)(2,1)} %param.23) | data formatting | bytes 65536 | tf_op args[5]
  2.2 0.0 copy-start
  2.2 2.0 %copy.20.qkvw_hbm = bf16[1024,192]{1,0:T(8,128)(2,1)} copy(bf16[1024,192]{0,1:T(8,128)(2,1)} %param.20) | data formatting | bytes 786432 | tf_op args[2]
  4.3 0.0 copy-done
  4.3 0.0 copy-start.1
  4.3 1.0 %copy.22.gatew_hbm = bf16[1024,176]{1,0:T(8,128)(2,1)} copy(bf16[1024,176]{0,1:T(8,128)(2,1)S(1)} %copy-done) | data formatting | bytes 720896 | tf_op args[15]
  5.3 0.0 copy-done.1
  5.3 1.0 %copy.23.upw_hbm = bf16[1024,176]{1,0:T(8,128)(2,1)} copy(bf16[1024,176]{0,1:T(8,128)(2,1)S(1)} %copy-done.1) | data formatting | bytes 720896 | tf_op args[16]
  6.3 69.8 %layer.1 = (bf16[2,1024]{1,0:T(2,128)(2,1)}, bf16[2,1024]{1,0:T(2,128)(2,1)}) custom-call(bf16[2,1024]{1,0:T(2,128)(2,1)} %tok_ref.1, f32[1,1024]{1,0:T(1,128)} %bitcast.5, bf16[1024,192]{1,0:T(8,128)(2,1)} %copy.20.qkvw_hbm, f32[4,192]{1,0:T(4,128)} %convw_ref.1, bf16[3,32,192]{2,1,0:T(8,128)(2,1)} %bitcast.4, bf16[1024,16]{1,0:T(8,128)(2,1)} %copy.21.mgate_ref, ...), custom_call_target="tpu_custom_call" | custom-call | tf_op jit(solution)/shard_map/layer/pallas_call | solution.py:428
  76.1 0.0 copy-start.2
  76.1 1.3 %copy.26 = bf16[2,1024]{1,0:T(2,128)(2,1)} copy(bf16[2,1024]{1,0:T(2,128)(2,1)} %get-tuple-element.4) | data formatting | bytes 8192
  77.4 0.0 copy-done.2
  77.4 0.6 copy.27
Async XLA Ops:
  2.2 2.0 %copy-start = (bf16[1024,176]{0,1:T(8,128)(2,1)S(1)}, bf16[1024,176]{0,1:T(8,128)(2,1)}, u32[]{:S(2)}) copy-start(bf16[1024,176]{0,1:T(8,128)(2,1)} %param.33) | copy-start | bytes 1081348
  4.3 1.0 %copy-start.1 = (bf16[1024,176]{0,1:T(8,128)(2,1)S(1)}, bf16[1024,176]{0,1:T(8,128)(2,1)}, u32[]{:S(2)}) copy-start(bf16[1024,176]{0,1:T(8,128)(2,1)} %param.34) | copy-start | bytes 1081348
  76.1 1.3 %copy-start.2 = (bf16[2,1024]{1,0:T(2,128)(2,1)S(1)}, bf16[2,1024]{1,0:T(2,128)(2,1)}, u32[]{:S(2)}) copy-start(bf16[2,1024]{1,0:T(2,128)(2,1)} %get-tuple-element.5) | copy-start | bytes 12292

commit v2 on v1

v2 whole, which is shorter than its diff:
```python
import functools

import jax
import jax.numpy as jnp
from jax import lax
from jax.experimental import pallas as pl
from jax.experimental.pallas import tpu as pltpu
from jax.sharding import PartitionSpec as P

MESH = pl.DeviceIdType.MESH
F32 = jnp.float32
BF16 = jnp.bfloat16
ITERS = 4


def iota(shape, dim):
    return lax.broadcasted_iota(jnp.int32, shape, dim)


def mm(a, b):
    return jnp.dot(a, b, preferred_element_type=F32)


def mm_nt(a, b):
    return lax.dot_general(a, b, (((1,), (1,)), ((), ())), preferred_element_type=F32)


def split(v):
    hi = v.astype(BF16)
    lo = (v - hi.astype(F32)).astype(BF16)
    return hi, lo


def silu(v):
    return v / (1.0 + jnp.exp(-v))


def row_norm(wide, gain):
    factor = lax.rsqrt(jnp.mean(wide * wide, axis=-1, keepdims=True) + 1e-05)
    return (wide * factor * gain).astype(BF16)


def unit_rows(v):
    return v * lax.rsqrt(jnp.sum(v * v, axis=-1, keepdims=True) + 1e-06)


def rowsum(v):
    return jnp.sum(v, axis=-1, keepdims=True)


def kernel(
    tok_ref, ngain_ref, qkvw_hbm, convw_ref, convs_hbm, mgate_ref, mbias_ref, ridge_ref,
    key_hbm, val_hbm, logw_ref, owner_ref, fill_ref, outw_hbm, mgain_ref, gatew_hbm, upw_hbm, downw_hbm,
    ret_ref, lay_ref,
    qkvw, convs, outw, gatew, upw, downw,
    kall, vall, tokall, xrows, wo_src, wo_all, wmask,
    usrc, uall, gall, ohd, ohall, ohs,
    csrc, call, rsrc, rall, fsrc, fall, tsrc, tall, nsrc, nall,
    lsem, osem, ssem, rsem,
):
    g = lax.axis_index("group")
    s = lax.axis_index("shard")
    par = g % 2
    base = g - par
    y = s // 2
    c = s % 2
    q = par * 2 + c

    def local(src, dst, sem):
        cp = pltpu.make_async_copy(src, dst, sem)
        cp.start()
        return cp

    def remote(src, dst, send, recv, dev):
        pltpu.make_async_remote_copy(
            src_ref=src, dst_ref=dst, send_sem=send, recv_sem=recv,
            device_id=dev, device_id_type=MESH,
        ).start()

    def done(ref, sem):
        pltpu.make_async_copy(ref, ref, sem).wait()

    def each(n, fn):
        def step(k, carry):
            fn(k)
            return carry
        lax.fori_loop(0, n, step, 0)

    def team(t):
        return base + t // 2, 2 * y + t % 2

    def line(k):
        return g, 2 * ((y + k) % 8) + c

    def pass_on(k):
        if k > 1:
            done(outw.at[pl.ds(0, 2), 0], rsem.at[16 + k])
        low, high = (y + 9 - k) % 8, (y + k - 1) % 8
        for way, at, to in ((0, low, 1), (1, high, 7)):
            rows = pl.ds(32 * way, 32) if k == 4 else pl.ds(0, 64)
            src = outw_hbm if k == 1 else outw.at[at, c, rows]
            remote(src, outw.at[at, c, rows], ssem.at[15 + k], rsem.at[17 + k], line(to))

    bar = pltpu.get_barrier_semaphore()
    rank = par * 16 + s

    def greet(k):
        to = (rank + k + 1) % 32
        pl.semaphore_signal(bar, inc=1, device_id=(base + to // 16, to % 16), device_id_type=MESH)

    each(31, greet)

    c_conv = local(convs_hbm, convs, lsem.at[0])
    c_qkv = local(qkvw_hbm, qkvw, lsem.at[1])
    mine = pl.ds(pl.multiple_of(q * 256, 256), 256)
    local(key_hbm.at[:, :, mine], kall.at[pl.ds(q * 4, 4)], rsem.at[0])
    c_gate = local(gatew_hbm, gatew, lsem.at[2])
    c_up = local(upw_hbm, upw, lsem.at[3])
    c_down = local(downw_hbm, downw, lsem.at[4])
    local(outw_hbm, outw.at[y, c], rsem.at[1])
    local(val_hbm.at[:, :, mine], vall.at[pl.ds(q * 4, 4)], rsem.at[2])
    local(tok_ref, tokall.at[s], rsem.at[3])

    row8 = iota((8, 128), 0)
    lane8 = iota((8, 128), 1)
    slot8 = row8 % 4

    def pick(ref):
        return jnp.where(
            slot8 == 0, ref[0], jnp.where(slot8 == 1, ref[1], jnp.where(slot8 == 2, ref[2], ref[3]))
        )

    live = lane8 < pick(fill_ref)
    own8 = pick(owner_ref).astype(F32)
    logw = logw_ref[...].astype(F32)
    for t in range(4):
        rows = [logw[j, 2 * t + h : 2 * t + h + 1, :] for h in range(2) for j in range(4)]
        wo_src[t, 0:8, :] = jnp.where(live, jnp.exp(jnp.concatenate(rows, axis=0)), 0.0)
        wo_src[t, 8:16, :] = own8
    c_conv.wait()
    past = jnp.zeros((32, 192), F32)
    for k in range(3):
        past = past + convw_ref[k : k + 1, :] * convs[k].astype(F32)

    pl.semaphore_wait(bar, 31)

    def send_tok(k):
        to = (s + k + 1) % 16
        remote(tok_ref, tokall.at[s], ssem.at[0], rsem.at[3], (g, to))

    each(15, send_tok)
    local(wo_src.at[q], wo_all.at[q], rsem.at[4])

    def send_wo(k):
        t = (q + k + 1) % 4
        remote(wo_src.at[t], wo_all.at[q], ssem.at[1], rsem.at[4], team(t))

    each(3, send_wo)

    def send_key(k):
        t = (q + k + 1) % 4
        cols = pl.ds(pl.multiple_of(t * 256, 256), 256)
        remote(key_hbm.at[:, :, cols], kall.at[pl.ds(q * 4, 4)], ssem.at[2], rsem.at[0], team(t))

    each(3, send_key)
    pass_on(1)

    c_qkv.wait()
    done(tokall, rsem.at[3])
    for i in range(16):
        xrows[2 * i : 2 * i + 2, :] = tokall[i].astype(F32)
    normed = row_norm(xrows[...], ngain_ref[...])
    fresh = mm_nt(normed, qkvw[...])
    pre = convw_ref[3:4, :] * fresh + past
    mixed = silu(pre).astype(BF16).astype(F32)
    lane16 = iota((16, 128), 1)
    low16 = lane16 < 64
    a = mixed[:, 0:128]
    b = mixed[:, 64:192]

    def fold(lower, upper):
        return jnp.where(low16, lower, upper).astype(BF16)

    usrc[0] = fold(a[0:16], pltpu.roll(a[16:32], 64, 1))
    usrc[1] = fold(pltpu.roll(a[0:16], 64, 1), a[16:32])
    usrc[2] = fold(pltpu.roll(b[0:16], 64, 1), b[16:32])
    for j in range(3):
        unit = 3 * s + j
        part = unit % 16
        tq = part // 4
        kind = unit // 16
        slot = kind * 8 + par * 4 + part % 4
        got = rsem.at[13 + kind]
        tg = base + tq // 2

        def send_unit(k, j=j, tq=tq, slot=slot, tg=tg, got=got):
            to = 2 * ((y + k + 1) % 8) + tq % 2
            remote(usrc.at[j], uall.at[slot], ssem.at[3], got, (tg, to))

        each(7, send_unit)

        @pl.when(tq == q)
        def _(j=j, slot=slot, got=got):
            local(usrc.at[j], uall.at[slot], got)

        @pl.when(tq != q)
        def _(j=j, slot=slot, tg=tg, tq=tq, got=got):
            remote(usrc.at[j], uall.at[slot], osem.at[j], got, (tg, 2 * y + tq % 2))

    gates = jax.nn.sigmoid(mm_nt(normed, mgate_ref[...]) + mbias_ref[...])
    gall[par, :, 0:16] = gates
    remote(gall.at[par], gall.at[par], ssem.at[4], rsem.at[6], (base + 1 - par, s))

    done(wo_all, rsem.at[4])
    row32 = iota((32, 128), 0)
    lane32 = iota((32, 128), 1)
    first = (row32 // 4) % 2 == 0
    own32 = wo_all[:, 8:16, :].reshape(32, 128)
    hot = (own32 == (lane32 % 64).astype(F32)) & ((row32 // 4) % 2 == lane32 // 64)
    ohd[...] = hot.astype(F32).astype(BF16)
    local(ohd, ohall.at[y], rsem.at[7])

    def send_oh(k):
        remote(ohd, ohall.at[y], ssem.at[5], rsem.at[7], line(k + 1))

    each(7, send_oh)
    w32 = wo_all[:, 0:8, :].reshape(32, 128)
    slot32 = (row32 // 8) * 4 + row32 % 4
    for p in range(16):
        wmask[:, 128 * p : 128 * p + 128] = jnp.where(slot32 == p, w32, 0.0)

    def send_val(k):
        t = (q + k + 1) % 4
        cols = pl.ds(pl.multiple_of(t * 256, 256), 256)
        remote(val_hbm.at[:, :, cols], vall.at[pl.ds(q * 4, 4)], ssem.at[6], rsem.at[2], team(t))

    each(3, send_val)

    pass_on(2)

    def unfold(kind):
        blocks = []
        for h in range(2):
            for p in range(2):
                left = uall[kind * 8 + p * 4 + 2 * h].astype(F32)
                right = uall[kind * 8 + p * 4 + 2 * h + 1].astype(F32)
                blocks.append(jnp.where(low16, left, pltpu.roll(right, 64, 1)))
                blocks.append(jnp.where(low16, pltpu.roll(left, 64, 1), right))
        return jnp.concatenate(blocks, axis=0)

    done(uall.at[pl.ds(0, 8)], rsem.at[13])
    query = unit_rows(unfold(0))
    done(kall, rsem.at[0])

    def spread(picked):
        return jnp.concatenate([jnp.where(first, picked, 0.0), jnp.where(first, 0.0, picked)], axis=1)

    def slot_rows(vec):
        hi, lo = split(vec)
        sel = mm(ohd[...], jnp.concatenate([hi, lo], axis=1))
        return jnp.concatenate([spread(sel[:, 0:128]), spread(sel[:, 128:256])], axis=0).astype(BF16)

    def weigh(scores):
        hi, lo = split((scores[0:32] + scores[32:64]) * wmask[...])
        return jnp.concatenate([hi, lo], axis=0)

    def gathered(prod):
        both = prod[0:32] + prod[32:64]
        return jnp.where(first, both[:, 0:128], both[:, 128:256]).astype(BF16)

    def own_term(vec, source):
        return strength * source * rowsum(knew * vec)

    def summed(part):
        return decay * mm(ohs[...], part.reshape(256, 128))

    keys = kall[...].reshape(2048, 256)
    solution = jnp.zeros((128, 128), F32)
    residual = query
    direction = query
    res_norm = rowsum(residual * residual)
    for it in range(ITERS):
        last = it == ITERS - 1
        src, dst = (fsrc, fall) if last else (csrc.at[it], call.at[it])
        weighed = weigh(mm_nt(slot_rows(direction), keys))
        src[0:32, :] = gathered(mm(weighed, keys))
        if last:
            values = vall[...].reshape(2048, 256)
            src[32:64, :] = gathered(mm(weighed, values))
        local(src, dst.at[y], rsem.at[8 + it])

        def send_c(k, it=it, src=src, dst=dst):
            remote(src, dst.at[y], ssem.at[8 + it], rsem.at[8 + it], line(k + 1))

        each(7, send_c)
        if it == 0:
            done(uall.at[pl.ds(8, 8)], rsem.at[14])
            knew = unit_rows(unfold(1))
            done(gall.at[0], rsem.at[6])
            gboth = gall[...].reshape(64, 128)
            lane64 = iota((64, 128), 1)

            def column(at):
                halves = [rowsum(jnp.where(lane64 == at + h, gboth, 0.0)) for h in range(2)]
                return jnp.concatenate(halves, axis=0)

            decay = column(2 * q)
            strength = column(8 + 2 * q)
            rowc = iota((128, 1), 0)
            ridge = jnp.where(rowc < 64, ridge_ref[2 * q], ridge_ref[2 * q + 1])
            done(ohall, rsem.at[7])
            ohs[...] = ohall[...].reshape(256, 128).astype(F32).T.astype(BF16)
            pass_on(3)
        if it == 1:
            pass_on(4)
            done(uall.at[pl.ds(16, 8)], rsem.at[15])
            vnew = unfold(2)
        if it == ITERS - 2:
            done(vall, rsem.at[2])
            values = vall[...].reshape(2048, 256)
            xweighed = weigh(mm_nt(slot_rows(solution), keys))
            reads = mm(jnp.concatenate([weighed, xweighed], axis=0), values)
            rsrc[0:32, :] = gathered(reads[0:64])
            rsrc[32:64, :] = gathered(reads[64:128])
            local(rsrc, rall.at[y], rsem.at[12])

            def send_r(k):
                remote(rsrc, rall.at[y], ssem.at[12], rsem.at[12], line(k + 1))

            each(7, send_r)
            done(outw.at[0, 0], rsem.at[1])
            done(outw.at[0, 0], rsem.at[21])
            remote(outw.at[:, c], outw.at[:, c], ssem.at[13], rsem.at[5], (g, 2 * y + 1 - c))
        near = own_term(direction, knew) + ridge * direction
        if last:
            done(rall, rsem.at[12])
            read_x = summed(rall[:, 32:64, :]) + step_size * summed(rall[:, 0:32, :])
            near_d = own_term(direction, vnew)
            near_x = own_term(solution, vnew)
        done(dst, rsem.at[8 + it])
        image = summed(dst[:, 0:32, :]) + near
        step_size = res_norm / rowsum(direction * image)
        if not last:
            solution = solution + step_size * direction
            residual = residual - step_size * image
            next_norm = rowsum(residual * residual)
            direction = residual + (next_norm / res_norm) * direction
            res_norm = next_norm
    found = (read_x + near_x + step_size * (summed(fall[:, 32:64, :]) + near_d)).astype(BF16)

    for p in range(2):
        for h in range(2):
            tsrc[p, h] = found[64 * h + 32 * p : 64 * h + 32 * p + 32, :]
    local(tsrc.at[par], tall.at[q], rsem.at[16])

    def send_t(k):
        t = (q + k + 1) % 4
        remote(tsrc.at[t // 2], tall.at[q], ssem.at[14], rsem.at[16], team(t))

    each(3, send_t)
    done(outw.at[:, c], rsem.at[5])
    done(tall, rsem.at[16])
    heads = jnp.concatenate([tall[h // 2, h % 2] for h in range(8)], axis=1)
    attended = mm(heads, outw[...].reshape(1024, 1024))
    mid = (xrows[...] + attended).astype(BF16)
    rows = row_norm(mid.astype(F32), mgain_ref[...])
    c_gate.wait()
    c_up.wait()
    c_down.wait()
    hidden = (silu(mm_nt(rows, gatew[...])) * mm_nt(rows, upw[...])).astype(BF16)
    down = mm(hidden, downw[...]).astype(BF16)
    for r in range(16):
        nsrc[r] = down[2 * r : 2 * r + 2, :]
    local(nsrc.at[s], nall.at[s], rsem.at[17])

    def send_n(k):
        to = (s + k + 1) % 16
        remote(nsrc.at[to], nall.at[s], ssem.at[15], rsem.at[17], (g, to))

    each(15, send_n)
    mine8 = (iota((8, 32), 1) == 2 * s + iota((8, 32), 0)).astype(F32).astype(BF16)
    ret_ref[...] = mm(mine8, heads)[0:2].astype(BF16)
    total = mm(mine8, mid)[0:2]
    done(nall, rsem.at[17])
    for i in range(16):
        total = total + nall[i].astype(F32)
    lay_ref[...] = total.astype(BF16)

    done(tokall.at[pl.ds(0, 15)], ssem.at[0])
    done(wo_all.at[pl.ds(0, 3)], ssem.at[1])
    done(kall.at[pl.ds(0, 12)], ssem.at[2])
    done(uall.at[pl.ds(0, 21)], ssem.at[3])
    done(gall.at[0], ssem.at[4])
    done(ohall.at[pl.ds(0, 7)], ssem.at[5])
    done(vall.at[pl.ds(0, 12)], ssem.at[6])
    for k in range(1, 5):
        done(outw.at[pl.ds(0, 1 if k == 4 else 2), 0], ssem.at[15 + k])
    for it in range(ITERS - 1):
        done(call.at[it, pl.ds(0, 7)], ssem.at[8 + it])
    done(fall.at[pl.ds(0, 7)], ssem.at[11])
    done(rall.at[pl.ds(0, 7)], ssem.at[12])
    done(outw.at[:, 0], ssem.at[13])
    done(tall.at[pl.ds(0, 3)], ssem.at[14])
    done(nall.at[pl.ds(0, 15)], ssem.at[15])
    for j in range(3):
        @pl.when(((3 * s + j) % 16) // 4 != q)
        def _(j=j):
            done(usrc.at[j], osem.at[j])


def body(
    tokens, norm_gain, qkv_weight, conv_weight, conv_state, mesa_gates, mesa_bias, ridge_term,
    key_cache, value_cache, log_weight, page_owner, page_fill, out_weight, mlp_gain,
    gate_weight, up_weight, down_weight,
):
    vm = pl.BlockSpec(memory_space=pltpu.VMEM)
    sm = pl.BlockSpec(memory_space=pltpu.SMEM)
    hb = pl.BlockSpec(memory_space=pltpu.HBM)
    v = pltpu.VMEM
    dma = pltpu.SemaphoreType.DMA
    return pl.pallas_call(
        kernel,
        name="layer",
        out_shape=(
            jax.ShapeDtypeStruct((2, 1024), BF16),
            jax.ShapeDtypeStruct((2, 1024), BF16),
        ),
        in_specs=[vm, vm, hb, vm, hb, vm, vm, sm, hb, hb, vm, sm, sm, hb, vm, hb, hb, hb],
        out_specs=(vm, vm),
        scratch_shapes=[
            v((192, 1024), BF16), v((3, 32, 192), BF16), v((8, 2, 64, 1024), BF16),
            v((176, 1024), BF16), v((176, 1024), BF16), v((176, 1024), BF16),
            v((16, 128, 256), BF16), v((16, 128, 256), BF16),
            v((16, 2, 1024), BF16), v((32, 1024), F32),
            v((4, 16, 128), F32), v((4, 16, 128), F32), v((32, 2048), F32),
            v((3, 16, 128), BF16), v((24, 16, 128), BF16), v((2, 32, 128), F32),
            v((32, 128), BF16), v((8, 32, 128), BF16), v((128, 256), BF16),
            v((3, 32, 128), BF16), v((3, 8, 32, 128), BF16),
            v((64, 128), BF16), v((8, 64, 128), BF16),
            v((64, 128), BF16), v((8, 64, 128), BF16),
            v((2, 2, 32, 128), BF16), v((4, 2, 32, 128), BF16),
            v((16, 2, 1024), BF16), v((16, 2, 1024), BF16),
            dma((5,)), dma((3,)), dma((20,)), dma((22,)),
        ],
        compiler_params=pltpu.CompilerParams(
            collective_id=0, has_side_effects=True, vmem_limit_bytes=56 * 1024 * 1024
        ),
    )(
        tokens, norm_gain.reshape(1, -1), qkv_weight.T, conv_weight, conv_state.transpose(1, 0, 2),
        mesa_gates.T, mesa_bias.reshape(1, -1), ridge_term, key_cache, value_cache, log_weight,
        page_owner, page_fill, out_weight, mlp_gain.reshape(1, -1), gate_weight.T, up_weight.T, down_weight,
    )


def solution(mesh):
    return jax.shard_map(
        body,
        mesh=mesh,
        in_specs=(
            P(("group", "shard"), None),
            P(),
            P(None, "shard"),
            P(None, "shard"),
            P("group", None, "shard"),
            P(),
            P(),
            P(),
            P(("group", "shard"), None, None),
            P(("group", "shard"), None, None),
            P(("group", "shard"), None, None),
            P(("group", "shard")),
            P(("group", "shard")),
            P("shard", None),
            P(),
            P(None, "shard"),
            P(None, "shard"),
            P("shard", None),
        ),
        out_specs=(P(("group", "shard"), None), P(("group", "shard"), None)),
        check_vma=False,
    )
```

time: 78.3 us -> 62.7 us (0.80)
  Pallas kernels: 69.8 us -> 59.9 us
  local copies, waits for them, and re-layouts: 7.53 us -> 1.87 us
    pallas_call x1, Pallas kernels: 69.8 us -> 59.9 us  [body(): pl.pallas_call(kernel, name='layer', out_shape=(jax.ShapeDtypeStruct((2,...]
    unnamed x12 -> x4, local copies, waits for them, and re-layouts: 7.53 us -> 1.87 us
where the time goes in v2:
time: 62.7 us; the launch traced here: 62.5 us
  Pallas kernels  59.9 us (96%)
  local copies, waits for them, and re-layouts  1.87 us (3%)
  between operations  0.65 us (1%)
    pallas_call x1, Pallas kernels, body(): pl.pallas_call(kernel, name='layer', out_shape=(jax.ShapeDtypeStruct((2,...  59.9 us
    unnamed x4, local copies, waits for them, and re-layouts  1.87 us

profile of v2, /device:TPU:1, one launch (start us, length us, event | category | flops | bytes accessed | tf_op | source)
XLA Modules:
  0.0 62.5 jit_solution(3831170493885656098)
XLA Ops:
  0.6 59.9 %layer.1 = (bf16[2,1024]{1,0:T(2,128)(2,1)}, bf16[2,1024]{1,0:T(2,128)(2,1)}) custom-call(bf16[2,1024]{1,0:T(2,128)(2,1)} %tok_ref.1, f32[1,1024]{1,0:T(1,128)} %bitcast.13, bf16[192,1024]{1,0:T(8,128)(2,1)} %bitcast.8, f32[4,192]{1,0:T(4,128)} %convw_ref.1, bf16[3,32,192]{2,1,0:T(8,128)(2,1)} %bitcast.11, bf16[16,1024]{1,0:T(8,128)(2,1)} %bitcast.12, ...), custom_call_target="tpu_custom_call" | custom-call | tf_op jit(solution)/shard_map/layer/pallas_call | solution.py:421
  60.6 0.0 copy-start
  60.6 1.3 %copy.22 = bf16[2,1024]{1,0:T(2,128)(2,1)} copy(bf16[2,1024]{1,0:T(2,128)(2,1)} %get-tuple-element.4) | data formatting | bytes 8192
  61.9 0.0 copy-done
  61.9 0.6 copy.23
Async XLA Ops:
  60.6 1.3 %copy-start = (bf16[2,1024]{1,0:T(2,128)(2,1)S(1)}, bf16[2,1024]{1,0:T(2,128)(2,1)}, u32[]{:S(2)}) copy-start(bf16[2,1024]{1,0:T(2,128)(2,1)} %get-tuple-element.5) | copy-start | bytes 12292

commit v3 on v0

v3 whole, which is shorter than its diff:
```python
import functools

import jax
import jax.numpy as jnp
from jax import lax
from jax.experimental import pallas as pl
from jax.experimental.pallas import tpu as pltpu
from jax.sharding import PartitionSpec as P

MESH = pl.DeviceIdType.MESH
F32 = jnp.float32
BF16 = jnp.bfloat16
ITERS = 4


def iota(shape, dim):
    return lax.broadcasted_iota(jnp.int32, shape, dim)


def mm(a, b):
    return jnp.dot(a, b, preferred_element_type=F32)


def mm_nt(a, b):
    return lax.dot_general(a, b, (((1,), (1,)), ((), ())), preferred_element_type=F32)


def split(v):
    hi = v.astype(BF16)
    lo = (v - hi.astype(F32)).astype(BF16)
    return hi, lo


def silu(v):
    return v / (1.0 + jnp.exp(-v))


def row_norm(wide, gain):
    factor = lax.rsqrt(jnp.mean(wide * wide, axis=-1, keepdims=True) + 1e-05)
    return (wide * factor * gain).astype(BF16)


def unit_rows(v):
    return v * lax.rsqrt(jnp.sum(v * v, axis=-1, keepdims=True) + 1e-06)


def rowsum(v):
    return jnp.sum(v, axis=-1, keepdims=True)


def kernel(
    tok_ref, ngain_ref, qkvw_hbm, convw_ref, convs_hbm, mgate_ref, mbias_ref, ridge_ref,
    key_hbm, val_hbm, logw_ref, owner_ref, fill_ref, outw_hbm, mgain_ref, gatew_hbm, upw_hbm, downw_hbm,
    ret_ref, lay_ref,
    qkvw, convs, outw, gatew, upw, downw,
    kall, vall, tokall, xrows, wo_src, wo_all, wmask, past_out, past_in,
    usrc, uall, gall, own_src, own_all, ohd, oht,
    csrc, call, rsrc, rall, fsrc, fall, tsrc, tall, nsrc, nall, hsrc, hall,
    kturn, lsem, osem, ssem, rsem,
):
    g = lax.axis_index("group")
    s = lax.axis_index("shard")
    par = g % 2
    base = g - par
    y = s // 2
    c = s % 2
    q = par * 2 + c
    partner = base + 1 - par

    def local(src, dst, sem):
        cp = pltpu.make_async_copy(src, dst, sem)
        cp.start()
        return cp

    def remote(src, dst, send, recv, dev):
        pltpu.make_async_remote_copy(
            src_ref=src, dst_ref=dst, send_sem=send, recv_sem=recv,
            device_id=dev, device_id_type=MESH,
        ).start()

    def done(ref, sem):
        pltpu.make_async_copy(ref, ref, sem).wait()

    def each(n, fn):
        def step(k, carry):
            fn(k)
            return carry
        lax.fori_loop(0, n, step, 0)

    def line(k):
        return g, 2 * ((y + k) % 8) + 1

    def heads_of(t):
        return pl.ds(pl.multiple_of(t * 512, 512), 512)

    slots = pl.ds(q * 4, 4)

    bar = pltpu.get_barrier_semaphore()
    rank = par * 16 + s

    def greet(k):
        to = c * ((rank + k + 1) % 32) + (1 - c) * ((2 * k + 1) % 32)
        pl.semaphore_signal(bar, inc=1, device_id=(base + to // 16, to % 16), device_id_type=MESH)

    each(16 + 15 * c, greet)

    c_conv = local(convs_hbm, convs, lsem.at[0])

    @pl.when(c == 1)
    def _():
        local(qkvw_hbm, qkvw.at[1], rsem.at[22])
        local(key_hbm.at[:, :, heads_of(par)], kall.at[slots], rsem.at[0])
        local(gatew_hbm, gatew.at[1], rsem.at[23])
        local(upw_hbm, upw.at[1], rsem.at[24])
        local(downw_hbm, downw.at[1], rsem.at[25])
        local(outw_hbm, outw.at[y, 1], rsem.at[1])
        local(val_hbm.at[:, :, heads_of(par)], vall.at[slots], rsem.at[2])
        local(tok_ref, tokall.at[s], rsem.at[3])

    slot16 = iota((16, 128), 0) % 4

    def pick(ref):
        return jnp.where(
            slot16 == 0, ref[0], jnp.where(slot16 == 1, ref[1], jnp.where(slot16 == 2, ref[2], ref[3]))
        )

    live = iota((16, 128), 1) < pick(fill_ref)
    own = pick(owner_ref).astype(F32)
    logw = logw_ref[...].astype(F32)
    for t in range(2):
        rows = [logw[j, 4 * t + h : 4 * t + h + 1, :] for h in range(4) for j in range(4)]
        wo_src[t, 0:16, :] = jnp.where(live, jnp.exp(jnp.concatenate(rows, axis=0)), 0.0)
        wo_src[t, 16:32, :] = own
    c_conv.wait()
    past = jnp.zeros((32, 192), F32)
    for k in range(3):
        past = past + convw_ref[k : k + 1, :] * convs[k].astype(F32)
    past_out[0:32, :] = past
    past_out[32:40, :] = jnp.broadcast_to(convw_ref[3:4, :], (8, 192))

    pl.semaphore_wait(bar, 16 + 15 * c)

    @pl.when(c == 0)
    def _():
        mate = (g, 2 * y + 1)

        def send_tok(k):
            remote(tok_ref, tokall.at[s], ssem.at[0], rsem.at[3], (g, 2 * ((y + k) % 8) + 1))

        each(8, send_tok)
        remote(past_out, past_in, ssem.at[3], rsem.at[5], mate)

        def send_wo(k):
            t = (par + k + 1) % 2
            remote(wo_src.at[t], wo_all.at[q], ssem.at[1], rsem.at[4], (base + t, 2 * y + 1))

        each(2, send_wo)

        def send_key(t):
            remote(key_hbm.at[:, :, heads_of(t)], kall.at[slots], ssem.at[2], rsem.at[0], (base + t, 2 * y + 1))

        def send_val(t):
            remote(val_hbm.at[:, :, heads_of(t)], vall.at[slots], ssem.at[6], rsem.at[2], (base + t, 2 * y + 1))

        send_key(1 - par)
        remote(qkvw_hbm, qkvw.at[0], ssem.at[4], rsem.at[22], mate)
        send_key(par)
        for to in (1, 7):
            remote(outw_hbm, outw.at[y, 0], ssem.at[5], rsem.at[18], line(to))
        remote(outw_hbm, outw.at[y, 0], ssem.at[7], rsem.at[1], mate)
        done(kall.at[pl.ds(0, 8)], ssem.at[2])
        send_val(1 - par)
        send_val(par)
        remote(gatew_hbm, gatew.at[0], ssem.at[8], rsem.at[23], mate)
        remote(upw_hbm, upw.at[0], ssem.at[9], rsem.at[24], mate)
        remote(downw_hbm, downw.at[0], ssem.at[10], rsem.at[25], mate)

    @pl.when(c == 1)
    def _():
        def pass_on(k):
            if k == 1:
                for to in (1, 7):
                    remote(outw_hbm, outw.at[y, 1], ssem.at[16], rsem.at[18], line(to))
                return
            done(outw.at[pl.ds(0, 2)], rsem.at[16 + k])
            if k == 2:
                done(outw.at[0], rsem.at[1])
            low, high = (y + 9 - k) % 8, (y + k - 1) % 8
            for way, at, to in ((0, low, 1), (1, high, 7)):
                rows = pl.ds(32 * way, 32) if k == 4 else pl.ds(0, 64)
                block = outw.at[at, :, rows]
                remote(block, block, ssem.at[15 + k], rsem.at[17 + k], line(to))

        def send_tok(k):
            remote(tok_ref, tokall.at[s], ssem.at[0], rsem.at[3], line(k + 1))

        each(7, send_tok)
        local(wo_src.at[par], wo_all.at[q], rsem.at[4])
        remote(wo_src.at[1 - par], wo_all.at[q], ssem.at[1], rsem.at[4], (partner, s))
        remote(key_hbm.at[:, :, heads_of(1 - par)], kall.at[slots], ssem.at[2], rsem.at[0], (partner, s))
        pass_on(1)

        done(wo_all, rsem.at[4])
        own16 = jnp.concatenate([wo_all[t, 16:20, :] for t in range(4)], axis=0)
        own_src[...] = own16.astype(BF16)
        local(own_src, own_all.at[y], rsem.at[7])

        def send_own(k):
            remote(own_src, own_all.at[y], ssem.at[5], rsem.at[7], line(k + 1))

        each(7, send_own)
        own64 = jnp.concatenate([own16] * 4, axis=0)
        lane256 = iota((64, 256), 1)
        hot = jnp.concatenate([own64, own64], axis=1) == (lane256 % 64).astype(F32)
        ohd[...] = (hot & (iota((64, 256), 0) // 16 == lane256 // 64)).astype(F32).astype(BF16)
        w64 = jnp.concatenate(
            [wo_all[t, 4 * h : 4 * h + 4, :] for h in range(4) for t in range(4)], axis=0
        )
        slot64 = iota((64, 128), 0) % 16
        for p in range(16):
            wmask[:, 128 * p : 128 * p + 128] = jnp.where(slot64 == p, w64, 0.0)

        done(past_in, rsem.at[5])
        low64 = iota((40, 128), 1) < 64
        left, right = past_in[...], past_out[...]
        taps = [
            left[:, 0:128],
            jnp.where(low64, pltpu.roll(left[:, 64:192], 64, 1), pltpu.roll(right[:, 0:128], 64, 1)),
            right[:, 64:192],
        ]

        done(qkvw, rsem.at[22])
        done(tokall, rsem.at[3])
        for i in range(16):
            xrows[2 * i : 2 * i + 2, :] = tokall[i].astype(F32)
        normed = row_norm(xrows[...], ngain_ref[...])
        fresh = mm_nt(normed, qkvw[...].reshape(384, 1024))
        for j in range(3):
            pre = taps[j][32:33] * fresh[:, 128 * j : 128 * j + 128] + taps[j][0:32]
            usrc[j] = silu(pre).astype(BF16)
        for j in range(3):
            unit = 3 * y + j
            kind = unit // 8
            head = unit % 8
            to_par = head // 4
            slot = kind * 8 + (head % 4) * 2 + par
            got = rsem.at[13 + kind]

            def send_unit(k, j=j, slot=slot, to_par=to_par, got=got):
                to = 2 * ((y + k + 1) % 8) + 1
                remote(usrc.at[j], uall.at[slot], ssem.at[3], got, (base + to_par, to))

            each(7, send_unit)

            @pl.when(to_par == par)
            def _(j=j, slot=slot, got=got):
                local(usrc.at[j], uall.at[slot], got)

            @pl.when(to_par != par)
            def _(j=j, slot=slot, got=got):
                remote(usrc.at[j], uall.at[slot], osem.at[j], got, (partner, s))

        gall[par, :, 0:16] = jax.nn.sigmoid(mm_nt(normed, mgate_ref[...]) + mbias_ref[...])
        remote(gall.at[par], gall.at[par], ssem.at[4], rsem.at[6], (partner, s))

        remote(val_hbm.at[:, :, heads_of(1 - par)], vall.at[slots], ssem.at[6], rsem.at[2], (partner, s))
        pass_on(2)

        def rows_of(kind):
            return uall[8 * kind : 8 * kind + 8].reshape(256, 128).astype(F32)

        done(uall.at[pl.ds(0, 8)], rsem.at[13])
        query = unit_rows(rows_of(0))
        done(kall, rsem.at[0])
        first = iota((32, 128), 0) < 16

        def spread(picked):
            return jnp.concatenate([jnp.where(first, picked, 0.0), jnp.where(first, 0.0, picked)], axis=1)

        def slot_rows(vec):
            hi, lo = split(vec)
            sel = mm(ohd[...], jnp.concatenate([hi, lo], axis=1))
            out = []
            for p in range(2):
                part = sel[32 * p : 32 * p + 32]
                both = [spread(part[:, 0:128]), spread(part[:, 128:256])]
                out.append(jnp.concatenate(both, axis=0).astype(BF16))
            return out

        def weigh(vec, turned=True):
            out = []
            for p, lhs in enumerate(slot_rows(vec)):
                scores = mm(lhs, kturn[p]) if turned else mm_nt(lhs, keys[p])
                hi, lo = split((scores[0:32] + scores[32:64]) * wmask[32 * p : 32 * p + 32, :])
                out.append(jnp.concatenate([hi, lo], axis=0))
            return out

        def gathered(weighed, source):
            out = []
            for p in range(2):
                prod = mm(weighed[p], source[p])
                both = prod[0:32] + prod[32:64]
                out.append(jnp.where(first, both[:, 0:128], both[:, 128:256]).astype(BF16))
            return jnp.concatenate(out, axis=0)

        def own_term(vec, source):
            return strength * source * rowsum(knew * vec)

        def summed(ref, at):
            wide = [ref[:, at + 16 * h : at + 16 * h + 16, :].reshape(128, 128) for h in range(4)]
            tot = mm(oht[...], jnp.concatenate(wide, axis=1))
            return decay * jnp.concatenate([tot[:, 128 * h : 128 * h + 128] for h in range(4)], axis=0)

        def halves(ref):
            return [ref[:, :, 256 * p : 256 * p + 256].reshape(2048, 256) for p in range(2)]

        keys = halves(kall)
        solution = jnp.zeros((256, 128), F32)
        residual = query
        direction = query
        res_norm = rowsum(residual * residual)
        for it in range(ITERS):
            last = it == ITERS - 1
            src, dst = (fsrc, fall) if last else (csrc.at[it], call.at[it])
            weighed = weigh(direction, it > 0)
            src[0:64, :] = gathered(weighed, keys)
            if last:
                src[64:128, :] = gathered(weighed, values)
            local(src, dst.at[y], rsem.at[8 + it])

            def send_c(k, it=it, src=src, dst=dst):
                remote(src, dst.at[y], ssem.at[8 + it], rsem.at[8 + it], line(k + 1))

            each(7, send_c)
            if it == 0:
                done(uall.at[pl.ds(8, 8)], rsem.at[14])
                knew = unit_rows(rows_of(1))
                done(gall.at[0], rsem.at[6])
                gboth = gall[...].reshape(64, 128)
                lane64 = iota((64, 128), 1)

                def column(at):
                    parts = [rowsum(jnp.where(lane64 == at + h, gboth, 0.0)) for h in range(4)]
                    return jnp.concatenate(parts, axis=0)

                decay = column(4 * par)
                strength = column(8 + 4 * par)
                ridge = jnp.concatenate(
                    [jnp.full((64, 1), ridge_ref[4 * par + h], F32) for h in range(4)], axis=0
                )
                done(own_all, rsem.at[7])
                owners = own_all[...].reshape(128, 128).astype(F32).T[0:64]
                oht[...] = (owners == iota((64, 128), 0).astype(F32)).astype(F32).astype(BF16)
                pass_on(3)
                for p in range(2):
                    for k in range(16):
                        kturn[p, :, 128 * k : 128 * k + 128] = kall[k, :, 256 * p : 256 * p + 256].T
            if it == 1:
                pass_on(4)
                done(uall.at[pl.ds(16, 8)], rsem.at[15])
                vnew = rows_of(2)
            if it == ITERS - 2:
                done(vall, rsem.at[2])
                values = halves(vall)
                rsrc[0:64, :] = gathered(weighed, values)
                rsrc[64:128, :] = gathered(weigh(solution), values)
                local(rsrc, rall.at[y], rsem.at[12])

                def send_r(k):
                    remote(rsrc, rall.at[y], ssem.at[12], rsem.at[12], line(k + 1))

                each(7, send_r)
            near = own_term(direction, knew) + ridge * direction
            if last:
                done(rall, rsem.at[12])
                read_x = summed(rall, 64) + step_size * summed(rall, 0)
                near_d = own_term(direction, vnew)
                near_x = own_term(solution, vnew)
            done(dst, rsem.at[8 + it])
            image = summed(dst, 0) + near
            step_size = res_norm / rowsum(direction * image)
            if not last:
                solution = solution + step_size * direction
                residual = residual - step_size * image
                next_norm = rowsum(residual * residual)
                direction = residual + (next_norm / res_norm) * direction
                res_norm = next_norm
        found = (read_x + near_x + step_size * (summed(fall, 64) + near_d)).astype(BF16)

        for p in range(2):
            for h in range(4):
                tsrc[p, h] = found[64 * h + 32 * p : 64 * h + 32 * p + 32, :]
        local(tsrc.at[par], tall.at[par], rsem.at[16])
        remote(tsrc.at[1 - par], tall.at[par], ssem.at[14], rsem.at[16], (partner, s))
        done(outw.at[0], rsem.at[21])
        done(gatew, rsem.at[23])
        done(upw, rsem.at[24])
        done(downw, rsem.at[25])
        done(tall, rsem.at[16])
        heads = jnp.concatenate([tall[h // 4, h % 4] for h in range(8)], axis=1)
        attended = mm(heads, outw[...].reshape(1024, 1024))
        mid = (xrows[...] + attended).astype(BF16)
        rows = row_norm(mid.astype(F32), mgain_ref[...])
        gate = mm_nt(rows, gatew[...].reshape(352, 1024))
        hidden = (silu(gate) * mm_nt(rows, upw[...].reshape(352, 1024))).astype(BF16)
        down = mm(hidden, downw[...].reshape(352, 1024)).astype(BF16)
        for r in range(16):
            nsrc[r] = down[2 * r : 2 * r + 2, :]
        local(nsrc.at[s], nall.at[y], rsem.at[17])

        def send_n(k):
            to = (s + k + 1) % 16
            remote(nsrc.at[to], nall.at[y], ssem.at[15], rsem.at[17], (g, to))

        each(15, send_n)
        chip = (iota((8, 32), 1) == 4 * y + iota((8, 32), 0)).astype(F32).astype(BF16)
        read4 = mm(chip, heads).astype(BF16)
        mid4 = mm(chip, mid)
        hsrc[0] = read4[0:2]
        hsrc[1] = mid4[0:2].astype(BF16)
        remote(hsrc, hall, ssem.at[20], rsem.at[26], (g, 2 * y))
        ret_ref[...] = read4[2:4]
        total = mid4[2:4]
        done(nall, rsem.at[17])
        for i in range(8):
            total = total + nall[i].astype(F32)
        lay_ref[...] = total.astype(BF16)

        done(tokall.at[pl.ds(0, 7)], ssem.at[0])
        done(wo_all.at[0], ssem.at[1])
        done(kall.at[pl.ds(0, 4)], ssem.at[2])
        done(uall.at[pl.ds(0, 21)], ssem.at[3])
        done(gall.at[0], ssem.at[4])
        done(own_all.at[pl.ds(0, 7)], ssem.at[5])
        done(vall.at[pl.ds(0, 4)], ssem.at[6])
        for it in range(ITERS - 1):
            done(call.at[it, pl.ds(0, 7)], ssem.at[8 + it])
        done(fall.at[pl.ds(0, 7)], ssem.at[11])
        done(rall.at[pl.ds(0, 7)], ssem.at[12])
        done(tall.at[0], ssem.at[14])
        done(nsrc.at[pl.ds(0, 15)], ssem.at[15])
        done(outw.at[0], ssem.at[16])
        done(outw.at[pl.ds(0, 2)], ssem.at[17])
        done(outw.at[pl.ds(0, 2)], ssem.at[18])
        done(outw.at[0], ssem.at[19])
        done(hsrc, ssem.at[20])
        for j in range(3):
            @pl.when(((3 * y + j) % 8) // 4 != par)
            def _(j=j):
                done(usrc.at[j], osem.at[j])

    @pl.when(c == 0)
    def _():
        done(hall, rsem.at[26])
        ret_ref[...] = hall[0]
        total = hall[1].astype(F32)
        done(nall, rsem.at[17])
        for i in range(8):
            total = total + nall[i].astype(F32)
        lay_ref[...] = total.astype(BF16)
        done(tokall.at[pl.ds(0, 8)], ssem.at[0])
        done(wo_all.at[pl.ds(0, 2)], ssem.at[1])
        done(past_out, ssem.at[3])
        done(qkvw.at[0], ssem.at[4])
        done(outw.at[0], ssem.at[5])
        done(vall.at[pl.ds(0, 8)], ssem.at[6])
        done(outw.at[0, 0], ssem.at[7])
        done(gatew.at[0], ssem.at[8])
        done(upw.at[0], ssem.at[9])
        done(downw.at[0], ssem.at[10])


def finish(read_ref, layer_ref, ret_ref, lay_ref):
    ret_ref[...] = read_ref[...]
    lay_ref[...] = layer_ref[...]


def body(
    tokens, norm_gain, qkv_weight, conv_weight, conv_state, mesa_gates, mesa_bias, ridge_term,
    key_cache, value_cache, log_weight, page_owner, page_fill, out_weight, mlp_gain,
    gate_weight, up_weight, down_weight,
):
    vm = pl.BlockSpec(memory_space=pltpu.VMEM)
    sm = pl.BlockSpec(memory_space=pltpu.SMEM)
    hb = pl.BlockSpec(memory_space=pltpu.HBM)
    v = pltpu.VMEM
    dma = pltpu.SemaphoreType.DMA
    pair = (jax.ShapeDtypeStruct((2, 1024), BF16), jax.ShapeDtypeStruct((2, 1024), BF16))
    read, layer = pl.pallas_call(
        kernel,
        name="layer",
        out_shape=pair,
        in_specs=[vm, vm, hb, vm, hb, vm, vm, sm, hb, hb, vm, sm, sm, hb, vm, hb, hb, hb],
        out_specs=(vm, vm),
        scratch_shapes=[
            v((2, 192, 1024), BF16), v((3, 32, 192), BF16), v((8, 2, 64, 1024), BF16),
            v((2, 176, 1024), BF16), v((2, 176, 1024), BF16), v((2, 176, 1024), BF16),
            v((16, 128, 512), BF16), v((16, 128, 512), BF16),
            v((16, 2, 1024), BF16), v((32, 1024), F32),
            v((2, 32, 128), F32), v((4, 32, 128), F32), v((64, 2048), F32),
            v((40, 192), F32), v((40, 192), F32),
            v((3, 32, 128), BF16), v((24, 32, 128), BF16), v((2, 32, 128), F32),
            v((16, 128), BF16), v((8, 16, 128), BF16), v((64, 256), BF16), v((64, 128), BF16),
            v((3, 64, 128), BF16), v((3, 8, 64, 128), BF16),
            v((128, 128), BF16), v((8, 128, 128), BF16),
            v((128, 128), BF16), v((8, 128, 128), BF16),
            v((2, 4, 32, 128), BF16), v((2, 4, 32, 128), BF16),
            v((16, 2, 1024), BF16), v((8, 2, 1024), BF16),
            v((2, 2, 1024), BF16), v((2, 2, 1024), BF16),
            v((2, 256, 2048), BF16),
            dma((1,)), dma((3,)), dma((21,)), dma((27,)),
        ],
        compiler_params=pltpu.CompilerParams(
            collective_id=0, has_side_effects=True, vmem_limit_bytes=56 * 1024 * 1024
        ),
    )(
        tokens, norm_gain.reshape(1, -1), qkv_weight.T, conv_weight, conv_state.transpose(1, 0, 2),
        mesa_gates.T, mesa_bias.reshape(1, -1), ridge_term, key_cache, value_cache, log_weight,
        page_owner, page_fill, out_weight, mlp_gain.reshape(1, -1), gate_weight.T, up_weight.T, down_weight,
    )
    return pl.pallas_call(
        finish, name="finish", out_shape=pair, in_specs=[vm, vm], out_specs=(vm, vm)
    )(read, layer)


def solution(mesh):
    return jax.shard_map(
        body,
        mesh=mesh,
        in_specs=(
            P(("group", "shard"), None),
            P(),
            P(None, "shard"),
            P(None, "shard"),
            P("group", None, "shard"),
            P(),
            P(),
            P(),
            P(("group", "shard"), None, None),
            P(("group", "shard"), None, None),
            P(("group", "shard"), None, None),
            P(("group", "shard")),
            P(("group", "shard")),
            P("shard", None),
            P(),
            P(None, "shard"),
            P(None, "shard"),
            P("shard", None),
        ),
        out_specs=(P(("group", "shard"), None), P(("group", "shard"), None)),
        check_vma=False,
    )
```

time: 784 us -> 60.4 us (0.08)
  waiting for transfers between devices: 539 us -> 0 us
  blocking collectives: 151 us -> 0 us
  Pallas kernels: 0 us -> 59.5 us
  starting transfers between devices: 37.7 us -> 0 us
  matrix products: 16.8 us -> 0 us
  between operations: 15.3 us -> 0.65 us
  other arithmetic: 14.5 us -> 0 us
  local copies, waits for them, and re-layouts: 9.11 us -> 0 us
    reduce_scatter x5 -> x0, waiting for transfers between devices: 289 us -> none  [reduce_home(): lax.psum_scatter(cache_pass(directions, decay_grp, with_values), 'shard',...]
    unnamed x9 -> x0, waiting for transfers between devices: 219 us -> none
    all_gather x8 -> x0, blocking collectives: 137 us -> none  [the longest x5 82.7 us: reduce_home(): lax.all_gather(vectors, 'shard', axis=0, tiled=True)]
    pallas_call x0 -> x2, Pallas kernels: none -> 59.5 us  [the longest x1 58.2 us: body(): pl.pallas_call(kernel, name='layer', out_shape=pair, in_specs=[vm, vm, hb...]
    ppermute x11 -> x0, starting transfers between devices: 34 us -> none  [partner(): return lax.ppermute(value, axis, pairs)]
    ppermute x11 -> x0, waiting for transfers between devices: 31.1 us -> none  [partner(): return lax.ppermute(value, axis, pairs)]
    dot_general x26 -> x0, matrix products: 16.8 us -> none  [the longest x5 4.65 us: slot_terms(): jnp.einsum('sht,sthd->shd', slot_weight * scores, source_wide, precision=...]
    all_to_all x1 -> x0, blocking collectives: 13.7 us -> none  [body(): lax.all_to_all(retrieved, 'shard', split_axis=1, concat_axis=0, tiled=True)]
  transfers between devices with their start and end apart: 19 -> 0, of which waited for: 17 -> 0; matrix products, arithmetic and copies ran while one was open for 1% -> 0% of each run, Pallas kernels for 0% -> 0%
where the time goes in v3:
time: 60.4 us; the launch traced here: 60.1 us
  Pallas kernels  59.5 us (99%)
  between operations  0.65 us (1%)
    pallas_call x1, Pallas kernels, body(): pl.pallas_call(kernel, name='layer', out_shape=pair, in_specs=[vm, vm, hb...  58.2 us
    pallas_call x1, Pallas kernels, body(): pl.pallas_call(finish, name='finish', out_shape=pair, in_specs=[vm, vm],...  1.3 us

profile of v3, /device:TPU:1, one launch (start us, length us, event | category | flops | bytes accessed | tf_op | source)
XLA Modules:
  0.0 60.1 jit_solution(15500742889533323133)
XLA Ops:
  0.6 58.2 %layer.1 = (bf16[2,1024]{1,0:T(2,128)(2,1)}, bf16[2,1024]{1,0:T(2,128)(2,1)}) custom-call(bf16[2,1024]{1,0:T(2,128)(2,1)} %tok_ref.1, f32[1,1024]{1,0:T(1,128)} %bitcast.13, bf16[192,1024]{1,0:T(8,128)(2,1)} %bitcast.8, f32[4,192]{1,0:T(4,128)} %convw_ref.1, bf16[3,32,192]{2,1,0:T(8,128)(2,1)} %bitcast.11, bf16[16,1024]{1,0:T(8,128)(2,1)} %bitcast.12, ...), custom_call_target="tpu_custom_call" | custom-call | tf_op jit(solution)/shard_map/layer/pallas_call | solution.py:489
  58.9 1.3 %finish.1 = (bf16[2,1024]{1,0:T(2,128)(2,1)}, bf16[2,1024]{1,0:T(2,128)(2,1)}) custom-call(bf16[2,1024]{1,0:T(2,128)(2,1)} %get-tuple-element.4.read_ref, bf16[2,1024]{1,0:T(2,128)(2,1)} %get-tuple-element.5.layer_ref), custom_call_target="tpu_custom_call" | custom-call | tf_op jit(solution)/shard_map/finish/pallas_call | solution.py:521

commit v4 on v3

--- a/solution.py
+++ b/solution.py
@@ -87,6 +87,9 @@
             return carry
         lax.fori_loop(0, n, step, 0)
 
+    def far(k):
+        return 4 + (k % 2) * ((k + 1) // 2) - (1 - k % 2) * (k // 2)
+
     def line(k):
         return g, 2 * ((y + k) % 8) + 1
 
@@ -145,7 +148,7 @@
         mate = (g, 2 * y + 1)
 
         def send_tok(k):
-            remote(tok_ref, tokall.at[s], ssem.at[0], rsem.at[3], (g, 2 * ((y + k) % 8) + 1))
+            remote(tok_ref, tokall.at[s], ssem.at[0], rsem.at[3], line(far(k)))
 
         each(8, send_tok)
         remote(past_out, past_in, ssem.at[3], rsem.at[5], mate)
@@ -192,7 +195,7 @@
                 remote(block, block, ssem.at[15 + k], rsem.at[17 + k], line(to))
 
         def send_tok(k):
-            remote(tok_ref, tokall.at[s], ssem.at[0], rsem.at[3], line(k + 1))
+            remote(tok_ref, tokall.at[s], ssem.at[0], rsem.at[3], line(far(k)))
 
         each(7, send_tok)
         local(wo_src.at[par], wo_all.at[q], rsem.at[4])
@@ -206,7 +209,7 @@
         local(own_src, own_all.at[y], rsem.at[7])
 
         def send_own(k):
-            remote(own_src, own_all.at[y], ssem.at[5], rsem.at[7], line(k + 1))
+            remote(own_src, own_all.at[y], ssem.at[5], rsem.at[7], line(far(k)))
 
         each(7, send_own)
         own64 = jnp.concatenate([own16] * 4, axis=0)
@@ -247,7 +250,7 @@
             got = rsem.at[13 + kind]
 
             def send_unit(k, j=j, slot=slot, to_par=to_par, got=got):
-                to = 2 * ((y + k + 1) % 8) + 1
+                to = 2 * ((y + far(k)) % 8) + 1
                 remote(usrc.at[j], uall.at[slot], ssem.at[3], got, (base + to_par, to))
 
             each(7, send_unit)
@@ -329,7 +332,7 @@
             local(src, dst.at[y], rsem.at[8 + it])
 
             def send_c(k, it=it, src=src, dst=dst):
-                remote(src, dst.at[y], ssem.at[8 + it], rsem.at[8 + it], line(k + 1))
+                remote(src, dst.at[y], ssem.at[8 + it], rsem.at[8 + it], line(far(k)))
 
             each(7, send_c)
             if it == 0:
@@ -367,7 +370,7 @@
                 local(rsrc, rall.at[y], rsem.at[12])
 
                 def send_r(k):
-                    remote(rsrc, rall.at[y], ssem.at[12], rsem.at[12], line(k + 1))
+                    remote(rsrc, rall.at[y], ssem.at[12], rsem.at[12], line(far(k)))
 
                 each(7, send_r)
             near = own_term(direction, knew) + ridge * direction
@@ -409,7 +412,7 @@
         local(nsrc.at[s], nall.at[y], rsem.at[17])
 
         def send_n(k):
-            to = (s + k + 1) % 16
+            to = 2 * ((y + far(k // 2)) % 8) + k % 2
             remote(nsrc.at[to], nall.at[y], ssem.at[15], rsem.at[17], (g, to))
 
         each(15, send_n)

time: 60.4 us -> 57.9 us (0.959)
  Pallas kernels: 59.5 us -> 57 us
    pallas_call x1, Pallas kernels: 58.2 us -> 55.7 us  [body(): pl.pallas_call(kernel, name='layer', out_shape=pair, in_specs=[vm, vm, hb...]
where the time goes in v4:
time: 57.9 us; the launch traced here: 57.6 us
  Pallas kernels  57 us (98%)
  between operations  0.65 us (1%)
    pallas_call x1, Pallas kernels, body(): pl.pallas_call(kernel, name='layer', out_shape=pair, in_specs=[vm, vm, hb...  55.7 us
    pallas_call x1, Pallas kernels, body(): pl.pallas_call(finish, name='finish', out_shape=pair, in_specs=[vm, vm],...  1.3 us

profile of v4, /device:TPU:1, one launch (start us, length us, event | category | flops | bytes accessed | tf_op | source)
XLA Modules:
  0.0 57.6 jit_solution(13348123357786970316)
XLA Ops:
  0.6 55.7 %layer.1 = (bf16[2,1024]{1,0:T(2,128)(2,1)}, bf16[2,1024]{1,0:T(2,128)(2,1)}) custom-call(bf16[2,1024]{1,0:T(2,128)(2,1)} %tok_ref.1, f32[1,1024]{1,0:T(1,128)} %bitcast.13, bf16[192,1024]{1,0:T(8,128)(2,1)} %bitcast.8, f32[4,192]{1,0:T(4,128)} %convw_ref.1, bf16[3,32,192]{2,1,0:T(8,128)(2,1)} %bitcast.11, bf16[16,1024]{1,0:T(8,128)(2,1)} %bitcast.12, ...), custom_call_target="tpu_custom_call" | custom-call | tf_op jit(solution)/shard_map/layer/pallas_call | solution.py:492
  56.3 1.3 %finish.1 = (bf16[2,1024]{1,0:T(2,128)(2,1)}, bf16[2,1024]{1,0:T(2,128)(2,1)}) custom-call(bf16[2,1024]{1,0:T(2,128)(2,1)} %get-tuple-element.4.read_ref, bf16[2,1024]{1,0:T(2,128)(2,1)} %get-tuple-element.5.layer_ref), custom_call_target="tpu_custom_call" | custom-call | tf_op jit(solution)/shard_map/finish/pallas_call | solution.py:524

commit v5 on v4

--- a/solution.py
+++ b/solution.py
@@ -241,6 +241,15 @@
         for j in range(3):
             pre = taps[j][32:33] * fresh[:, 128 * j : 128 * j + 128] + taps[j][0:32]
             usrc[j] = silu(pre).astype(BF16)
+        def send_units(k):
+            to = 2 * ((y + far(k)) % 8) + 1
+            for j in range(3):
+                unit = 3 * y + j
+                head = unit % 8
+                slot = (unit // 8) * 8 + (head % 4) * 2 + par
+                remote(usrc.at[j], uall.at[slot], ssem.at[3], rsem.at[13 + unit // 8], (base + head // 4, to))
+
+        each(7, send_units)
         for j in range(3):
             unit = 3 * y + j
             kind = unit // 8
@@ -248,12 +257,6 @@
             to_par = head // 4
             slot = kind * 8 + (head % 4) * 2 + par
             got = rsem.at[13 + kind]
-
-            def send_unit(k, j=j, slot=slot, to_par=to_par, got=got):
-                to = 2 * ((y + far(k)) % 8) + 1
-                remote(usrc.at[j], uall.at[slot], ssem.at[3], got, (base + to_par, to))
-
-            each(7, send_unit)
 
             @pl.when(to_par == par)
             def _(j=j, slot=slot, got=got):

time: 57.9 us -> 57.7 us (level)
  no operation moved by 1% of the time
where the time goes in v5:
time: 57.7 us; the launch traced here: 57.5 us
  Pallas kernels  56.8 us (98%)
  between operations  0.65 us (1%)
    pallas_call x1, Pallas kernels, body(): pl.pallas_call(kernel, name='layer', out_shape=pair, in_specs=[vm, vm, hb...  55.5 us
    pallas_call x1, Pallas kernels, body(): pl.pallas_call(finish, name='finish', out_shape=pair, in_specs=[vm, vm],...  1.3 us

profile of v5, /device:TPU:1, one launch (start us, length us, event | category | flops | bytes accessed | tf_op | source)
XLA Modules:
  0.0 57.5 jit_solution(11724271665758738928)
XLA Ops:
  0.6 55.5 %layer.1 = (bf16[2,1024]{1,0:T(2,128)(2,1)}, bf16[2,1024]{1,0:T(2,128)(2,1)}) custom-call(bf16[2,1024]{1,0:T(2,128)(2,1)} %tok_ref.1, f32[1,1024]{1,0:T(1,128)} %bitcast.13, bf16[192,1024]{1,0:T(8,128)(2,1)} %bitcast.8, f32[4,192]{1,0:T(4,128)} %convw_ref.1, bf16[3,32,192]{2,1,0:T(8,128)(2,1)} %bitcast.11, bf16[16,1024]{1,0:T(8,128)(2,1)} %bitcast.12, ...), custom_call_target="tpu_custom_call" | custom-call | tf_op jit(solution)/shard_map/layer/pallas_call | solution.py:495
  56.2 1.3 %finish.1 = (bf16[2,1024]{1,0:T(2,128)(2,1)}, bf16[2,1024]{1,0:T(2,128)(2,1)}) custom-call(bf16[2,1024]{1,0:T(2,128)(2,1)} %get-tuple-element.4.read_ref, bf16[2,1024]{1,0:T(2,128)(2,1)} %get-tuple-element.5.layer_ref), custom_call_target="tpu_custom_call" | custom-call | tf_op jit(solution)/shard_map/finish/pallas_call | solution.py:527
